TPU v7x, 256 devices: a whole 4x4x8 slice. The times are simulated.
256 devices in a mesh: win: 16 (over y, z_lo), space: 16 (over z_hi, x, core).
Axes of the slice: x: 4, y: 4, z: 8 (z_hi: 2, z_lo: 4; z = z_hi * 4 + z_lo), core: 2. Of those that a mesh axis runs over, the one named last changes fastest.
Arguments:
- increment: float32 [16, 64, 256, 256], P('win', 'space'), may hold values from -6 to 6
- multiplier: float32 [16, 64, 256, 256], P('win', 'space'), may hold values from -6 to 6
- obs_dual: float32 [16, 16384], P('win', 'space'), may hold values from -6 to 6
- obs_sites: int32 [16, 3, 16384], P('win'), may hold values from 0 to 255, as said below
- obs_variance: float32 [16, 16384], P('win', 'space'), may hold values from 0.5 to 2
- trajectory: bfloat16 [16, 64, 256, 256], P('win', None, 'space'), may hold values from -6 to 6
- diffusion: float32 [64], replicated, may hold values from 0.05 to 0.2
- drift_rows: float32 [64], replicated, may hold values from -0.25 to 0.25
- drift_cols: float32 [64], replicated, may hold values from -0.25 to 0.25
- spread: float32 [64], replicated, may hold values from 0.5 to 2
- row_factor: float32 [256, 256], replicated, may hold values from -0.375 to 0.375
- col_factor: float32 [256, 256], replicated, may hold values from -0.375 to 0.375
- layer_in: bfloat16 [1024, 64], replicated, may hold values from -0.75 to 0.75
- bias_in: float32 [1024], replicated, may hold values from -4 to 4
- layer_out: bfloat16 [64, 1024], replicated, may hold values from -0.1875 to 0.1875
Outputs:
- state_out: float32 [16, 64, 256, 256], P('win', 'space')
- obs_out: float32 [16, 16384], P('win', 'space')
- mult_out: float32 [16, 64, 256, 256], P('win', 'space')
Inputs may be any that keep to these rules, and one draw needn't show every extreme that they name: `obs_sites`: row 0 holds a level below 64, row 1 a first index below 256, row 2 a second index below 256; positions may repeat.
All inputs are finite; a program needn't handle non-finite values.
Results may differ from a plain program's by a relative error of at most 0.0011.
Values sent between devices are 32-bit elements; how exact they have to be, the bound alone decides.
A program may use at most 64 MiB of HBM per device.

v0:
```python
import jax
import jax.numpy as jnp
from jax import lax
from jax.sharding import PartitionSpec as P

STEPS = 4


exact_mode = lax.Precision.HIGHEST


def from_behind(value, axis, steps):
    count = lax.axis_size(axis)
    first, last = (max(0, -steps), min(count, count - steps))
    return lax.ppermute(value, axis, [(source, source + steps) for source in range(first, last)])


def side_by_side(arrays, axis, split_dim, concat_dim, along):
    ends, at = ([], 0)
    for a in arrays[:-1]:
        at += a.shape[along]
        ends.append(at)
    both = jnp.concatenate(arrays, axis=along)
    return tuple(
        jnp.split(
            lax.all_to_all(both, axis, split_axis=split_dim, concat_axis=concat_dim, tiled=True),
            ends,
            axis=along,
        )
    )


def split_up(value, dim, count):
    before, after = (value.shape[:dim], value.shape[dim + 1 :])
    return jnp.moveaxis(value.reshape(*before, count, -1, *after), dim, 0)


def summed_on_arrival(value, axis, dim):
    count = lax.axis_size(axis)
    tiles = lax.all_to_all(split_up(value, dim, count), axis, 0, 0, tiled=True)
    return jnp.sum(tiles, axis=0)


def stencil_step(padded, diffusion, drift_rows, drift_cols, direction):
    centre = padded[:, 1:-1, :]
    row_up = padded[:, 2:, :]
    row_down = padded[:, :-2, :]
    widened = jnp.pad(centre, ((0, 0), (0, 0), (1, 1)))
    col_up = widened[:, :, 2:]
    col_down = widened[:, :, :-2]
    mixing = row_up + row_down + col_up + col_down - 4.0 * centre
    carried = drift_rows * (row_up - row_down) + drift_cols * (col_up - col_down)
    return centre + diffusion * mixing - direction * carried


def network_both(forward_in, backward_in, trajectory, layer_in, bias_in, layer_out):
    levels, row_count, columns = forward_in.shape
    block_rows = min(row_count, max(1, 1024 // columns))

    def select(source, first_row):
        piece = lax.dynamic_slice_in_dim(source, first_row, block_rows, 1)
        return piece.reshape(levels, block_rows * columns)

    def visit(block_index, totals):
        first_row = (block_index * block_rows).astype(jnp.int32)
        path = select(trajectory, first_row)
        activation = jnp.dot(layer_in, path, preferred_element_type=jnp.float32) + bias_in[:, None]
        gating = jax.nn.sigmoid(activation)
        slopes = gating * (1.0 + activation * (1.0 - gating))
        tangent_in = select(forward_in, first_row)
        hidden = (
            slopes
            * jnp.dot(layer_in, tangent_in.astype(jnp.bfloat16), preferred_element_type=jnp.float32)
        ).astype(jnp.bfloat16)
        tangent_out = tangent_in + jnp.dot(layer_out, hidden, preferred_element_type=jnp.float32)
        adjoint_in = select(backward_in, first_row)
        back_hidden = (
            slopes
            * jnp.dot(
                layer_out.T, adjoint_in.astype(jnp.bfloat16), preferred_element_type=jnp.float32
            )
        ).astype(jnp.bfloat16)
        adjoint_out = adjoint_in + jnp.dot(
            layer_in.T, back_hidden, preferred_element_type=jnp.float32
        )
        shape = (levels, block_rows, columns)
        return (
            lax.dynamic_update_slice_in_dim(totals[0], tangent_out.reshape(shape), first_row, 1),
            lax.dynamic_update_slice_in_dim(totals[1], adjoint_out.reshape(shape), first_row, 1),
        )

    empty = jnp.zeros(forward_in.shape, jnp.float32)
    return lax.fori_loop(0, row_count // block_rows, visit, (empty, empty))


def correlate(fields, spread, row_factor, col_factor):
    inner = jnp.einsum("xa,lxy->lay", row_factor, fields, precision=exact_mode)
    inner = jnp.einsum("lay,yb->lab", inner, col_factor, precision=exact_mode)
    outer = jnp.einsum("xa,lab->lxb", row_factor, inner, precision=exact_mode)
    outer = jnp.einsum("lxb,yb->lxy", outer, col_factor, precision=exact_mode)
    return (spread * spread)[:, None, None] * outer


def slab_steps(fields, coefs, direction):
    for repeat in range(STEPS):
        padded = jnp.pad(fields, ((0, 0), (1, 1), (0, 0)))
        fields = stencil_step(padded, coefs[0], coefs[1], coefs[2], direction)
    return fields


def body(
    increment,
    multiplier,
    obs_dual,
    obs_sites,
    obs_variance,
    trajectory,
    diffusion,
    drift_rows,
    drift_cols,
    spread,
    row_factor,
    col_factor,
    layer_in,
    bias_in,
    layer_out,
):
    level_count = increment.shape[1]
    grid_rows = increment.shape[2]
    grid_cols = increment.shape[3]
    space_index = lax.axis_index("space")
    level_first = space_index * level_count

    def local_coefs(values):
        return lax.dynamic_slice_in_dim(values, level_first, level_count)[:, None, None]

    slab_coefs = (local_coefs(diffusion), local_coefs(drift_rows), local_coefs(drift_cols))
    own_state = increment[0]
    own_mult = multiplier[0]
    previous = from_behind(own_state, "win", 1)
    outgoing = slab_steps(previous, slab_coefs, 1.0)
    strip_state, strip_mult = side_by_side((outgoing, own_mult), "space", 1, 0, 2)
    forward, backward = network_both(
        strip_state, strip_mult, trajectory[0], layer_in, bias_in, layer_out
    )
    slab_forward, slab_backward = side_by_side((forward, backward), "space", 0, 1, 2)
    slab_backward = slab_steps(slab_backward, slab_coefs, -1.0)
    later = from_behind(slab_backward, "win", -1)
    local_spread = lax.dynamic_slice_in_dim(spread, level_first, level_count)
    correlated = correlate(own_mult, local_spread, row_factor, col_factor)
    state_out = correlated + own_state - slab_forward
    duals = lax.all_gather(obs_dual[0], "space", axis=0, tiled=True)
    positions = obs_sites[0]
    local_level = positions[0] - level_first
    inside = (local_level >= 0) & (local_level < level_count)
    row_total = level_count * grid_rows
    row_index = jnp.where(inside, local_level * grid_rows + positions[1], row_total)
    block_size = obs_dual.shape[1]
    block_count = positions.shape[1] // block_size
    index_blocks = row_index.reshape(block_count, block_size)
    column_blocks = positions[2].reshape(block_count, block_size)
    dual_blocks = duals.reshape(block_count, block_size)
    flat_state = own_state.reshape(row_total, grid_cols)
    column_ids = lax.iota(jnp.int32, grid_cols)[None, :]

    def pick_block(block_items):
        block_rows_index, block_columns = block_items
        picked = jnp.take(flat_state, block_rows_index, axis=0, mode="fill", fill_value=0.0)
        chosen = column_ids == block_columns[:, None]
        return jnp.sum(jnp.where(chosen, picked, 0.0), axis=1)

    seen = lax.map(pick_block, (index_blocks, column_blocks)).reshape(-1)
    partial_value = summed_on_arrival(seen, "space", 0)
    obs_out = obs_variance[0] * obs_dual[0] + partial_value

    def add_block(block_number, total):
        block_rows_index = index_blocks[block_number]
        chosen = column_ids == column_blocks[block_number][:, None]
        spread_rows = jnp.where(chosen, dual_blocks[block_number][:, None], 0.0)
        return total.at[block_rows_index].add(spread_rows, mode="drop")

    placed_rows = lax.fori_loop(
        0, block_count, add_block, jnp.zeros((row_total, grid_cols), jnp.float32)
    )
    placed = placed_rows.reshape(level_count, grid_rows, grid_cols)
    mult_out = own_mult - later + placed
    return (state_out[None], obs_out[None], mult_out[None])


def solution(mesh):
    placed = (
        P("win", "space", None, None),
        P("win", "space", None, None),
        P("win", "space"),
        P("win", None, None),
        P("win", "space"),
        P("win", None, "space", None),
        P(),
        P(),
        P(),
        P(),
        P(),
        P(),
        P(),
        P(),
        P(),
    )
    return jax.shard_map(
        body,
        mesh=mesh,
        in_specs=placed,
        out_specs=(P("win", "space", None, None), P("win", "space"), P("win", "space", None, None)),
        check_vma=False,
    )
```

profile of v0, /device:TPU:25, one launch (start us, length us, event | category | flops | bytes accessed | tf_op | source)
XLA Modules:
  0.0 424.3 jit_solution(580370550137409803)
XLA Ops:
  0.6 3.7 collective-permute-start
  7.9 22.4 %collective-permute-done = f32[4,256,256]{2,1,0:T(8,128)S(1)} collective-permute-done((f32[4,256,256]{2,1,0:T(8,128)}, f32[4,256,256]{2,1,0:T(8,128)S(1)}, u32[]{:S(2)}, u32[]{:S(2)}) %collective-permute-start) | collective-permute-done | bytes 1048608 | tf_op jit(solution)/shard_map/ppermute | solution.py:15
  35.6 2.7 copy.26
  38.3 11.9 %all-to-all-start = ((f32[4,256,512]{2,0,1:T(4,128)}), f32[4,256,512]{2,0,1:T(4,128)}, u32[]{:S(2)}, u32[]{:S(2)}) async-start(f32[4,256,512]{2,0,1:T(4,128)} %copy.26), calls=%async_computation | async-start | bytes 4194304 | tf_op jit(solution)/shard_map/all_to_all | solution.py:26
  50.3 87.0 %while.41 = (s32[]{:T(128)}, f32[16,1024]{1,0:T(8,128)}, s32[16,1024]{1,0:T(8,128)S(1)}, s32[16,1024]{1,0:T(8,128)S(1)}, f32[1024,256]{1,0:T(8,128)S(1)}, /*index=5*/s32[]{:T(128)}, s32[]{:T(128)}) while((s32[]{:T(128)}, f32[16,1024]{1,0:T(8,128)}, s32[16,1024]{1,0:T(8,128)S(1)}, s32[16,1024]{1,0:T(8,128)S(1)}, ...), condition=%wide.region_4.5_spmd.clone, body=%wide.region_2.4_spmd.clone.sunk | while | flops 1057794 | bytes 3201113 | solution.py:172
  50.3 3.5 gather_fusion
  55.8 3.5 gather_fusion
  61.2 3.5 gather_fusion
  66.6 3.5 gather_fusion
  72.1 3.5 gather_fusion
  77.5 3.5 gather_fusion
  82.9 3.5 gather_fusion
  88.4 3.5 gather_fusion
  93.8 3.5 gather_fusion
  99.3 3.5 gather_fusion
  104.7 3.5 gather_fusion
  110.1 3.5 gather_fusion
  115.6 3.5 gather_fusion
  121.0 3.5 gather_fusion
  126.4 3.5 gather_fusion
  131.9 3.5 gather_fusion
  137.3 31.9 %all-gather = f32[1,16384]{1,0:T(1,128)S(1)} all-gather(f32[1,1024]{1,0:T(1,128)S(1)} %copy-done.14), channel_id=2, replica_groups=mesh['win'=16,'space'=16] {'space'}, dimensions={1}, use_global_device_ids=true | all-gather | bytes 69632 | tf_op jit(solution)/shard_map/all_gather | solution.py:152
  172.7 2.8 convolution_bitcast_fusion.1
  175.5 2.3 copy.27
  177.7 1.6 fusion.36
  181.6 60.5 %while.40 = (s32[]{:T(128)}, f32[64,16,256]{2,1,0:T(8,128)}, f32[64,16,256]{2,1,0:T(8,128)}, f32[64,16,256]{2,1,0:T(8,128)}, bf16[64,16,256]{2,1,0:T(8,128)(2,1)...) while((s32[]{:T(128)}, f32[64,16,256]{2,1,0:T(8,128)}, ...), condition=%wide.region_1.2_spmd, body=%wide.region_0.1_spmd.sunk | while | flops 683933696 | bytes 19140796 | solution.py:93
  182.7 3.6 fusion.66
  187.5 3.5 fusion.68
  192.2 3.5 fusion.67
  197.8 3.6 fusion.66
  202.6 3.5 fusion.68
  207.3 3.5 fusion.67
  212.9 3.6 fusion.66
  217.7 3.5 fusion.68
  222.5 3.5 fusion.67
  228.0 3.6 fusion.66
  232.8 3.5 fusion.68
  237.6 3.5 fusion.67
  242.1 3.2 pad_maximum_fusion.1
  245.3 4.3 %all-to-all-start.1 = ((f32[64,16,512]{2,1,0:T(8,128)}), f32[64,16,512]{2,1,0:T(8,128)}, u32[]{:S(2)}, u32[]{:S(2)}) async-start(f32[64,16,512]{2,1,0:T(8,128)} %pad_maximum_fusion.1), calls=%async_computation.1 | async-start | bytes 4194304 | tf_op jit(solution)/shard_map/all_to_all | solution.py:26
  249.7 126.9 %while.42 = (s32[]{:T(128)}, f32[1024,256]{1,0:T(8,128)S(1)}, s32[16,1024]{1,0:T(8,128)S(1)}, s32[16,1024]{1,0:T(8,128)S(1)}, f32[16,1024]{1,0:T(8,128)}, /*index=5*/s32[]{:T(128)}, f32[]{:T(128)}) while((s32[]{:T(128)}, f32[1024,256]{1,0:T(8,128)S(1)}, s32[16,1024]{1,0:T(8,128)S(1)}, s32[16,1024]{1,0:T(8,128)S(1)}, ...), condition=%wide.region_8.9_spmd.clone, body=%wide.region_6.8_spmd.clone.sunk | while | flops 789506 | bytes 1081437 | solution.py:182
  250.6 7.1 %scatter_custom_fusion.6 = f32[1024,256]{1,0:T(8,128)S(1)} fusion(f32[1024,256]{1,0:T(8,128)S(1)} %get-tuple-element.566, s32[1024]{0:T(1024)S(1)} %bitcast.177, f32[]{:T(128)} %constant.116.clone.1..sunk, f32[1024]{0:T(1024)S(1)} %bitcast.172, s32[1024]{0:T(1024)S(1)} %bitcast.173), kind=kCustom, calls=%fused_computation.37.clone.1 | custom fusion | flops 786432 | bytes 1056772 | tf_op jit(solution)/shard_map/while/body/eval_jaxpr/scatter-add | solution.py:180
  258.5 7.1 %scatter_custom_fusion.6 = f32[1024,256]{1,0:T(8,128)S(1)} fusion(f32[1024,256]{1,0:T(8,128)S(1)} %get-tuple-element.566, s32[1024]{0:T(1024)S(1)} %bitcast.177, f32[]{:T(128)} %constant.116.clone.1..sunk, f32[1024]{0:T(1024)S(1)} %bitcast.172, s32[1024]{0:T(1024)S(1)} %bitcast.173), kind=kCustom, calls=%fused_computation.37.clone.1 | custom fusion | flops 786432 | bytes 1056772 | tf_op jit(solution)/shard_map/while/body/eval_jaxpr/scatter-add | solution.py:180
  266.4 7.1 %scatter_custom_fusion.6 = f32[1024,256]{1,0:T(8,128)S(1)} fusion(f32[1024,256]{1,0:T(8,128)S(1)} %get-tuple-element.566, s32[1024]{0:T(1024)S(1)} %bitcast.177, f32[]{:T(128)} %constant.116.clone.1..sunk, f32[1024]{0:T(1024)S(1)} %bitcast.172, s32[1024]{0:T(1024)S(1)} %bitcast.173), kind=kCustom, calls=%fused_computation.37.clone.1 | custom fusion | flops 786432 | bytes 1056772 | tf_op jit(solution)/shard_map/while/body/eval_jaxpr/scatter-add | solution.py:180
  274.4 7.1 %scatter_custom_fusion.6 = f32[1024,256]{1,0:T(8,128)S(1)} fusion(f32[1024,256]{1,0:T(8,128)S(1)} %get-tuple-element.566, s32[1024]{0:T(1024)S(1)} %bitcast.177, f32[]{:T(128)} %constant.116.clone.1..sunk, f32[1024]{0:T(1024)S(1)} %bitcast.172, s32[1024]{0:T(1024)S(1)} %bitcast.173), kind=kCustom, calls=%fused_computation.37.clone.1 | custom fusion | flops 786432 | bytes 1056772 | tf_op jit(solution)/shard_map/while/body/eval_jaxpr/scatter-add | solution.py:180
  282.3 7.1 %scatter_custom_fusion.6 = f32[1024,256]{1,0:T(8,128)S(1)} fusion(f32[1024,256]{1,0:T(8,128)S(1)} %get-tuple-element.566, s32[1024]{0:T(1024)S(1)} %bitcast.177, f32[]{:T(128)} %constant.116.clone.1..sunk, f32[1024]{0:T(1024)S(1)} %bitcast.172, s32[1024]{0:T(1024)S(1)} %bitcast.173), kind=kCustom, calls=%fused_computation.37.clone.1 | custom fusion | flops 786432 | bytes 1056772 | tf_op jit(solution)/shard_map/while/body/eval_jaxpr/scatter-add | solution.py:180
  290.2 7.1 %scatter_custom_fusion.6 = f32[1024,256]{1,0:T(8,128)S(1)} fusion(f32[1024,256]{1,0:T(8,128)S(1)} %get-tuple-element.566, s32[1024]{0:T(1024)S(1)} %bitcast.177, f32[]{:T(128)} %constant.116.clone.1..sunk, f32[1024]{0:T(1024)S(1)} %bitcast.172, s32[1024]{0:T(1024)S(1)} %bitcast.173), kind=kCustom, calls=%fused_computation.37.clone.1 | custom fusion | flops 786432 | bytes 1056772 | tf_op jit(solution)/shard_map/while/body/eval_jaxpr/scatter-add | solution.py:180
  298.1 7.1 %scatter_custom_fusion.6 = f32[1024,256]{1,0:T(8,128)S(1)} fusion(f32[1024,256]{1,0:T(8,128)S(1)} %get-tuple-element.566, s32[1024]{0:T(1024)S(1)} %bitcast.177, f32[]{:T(128)} %constant.116.clone.1..sunk, f32[1024]{0:T(1024)S(1)} %bitcast.172, s32[1024]{0:T(1024)S(1)} %bitcast.173), kind=kCustom, calls=%fused_computation.37.clone.1 | custom fusion | flops 786432 | bytes 1056772 | tf_op jit(solution)/shard_map/while/body/eval_jaxpr/scatter-add | solution.py:180
  306.1 7.1 %scatter_custom_fusion.6 = f32[1024,256]{1,0:T(8,128)S(1)} fusion(f32[1024,256]{1,0:T(8,128)S(1)} %get-tuple-element.566, s32[1024]{0:T(1024)S(1)} %bitcast.177, f32[]{:T(128)} %constant.116.clone.1..sunk, f32[1024]{0:T(1024)S(1)} %bitcast.172, s32[1024]{0:T(1024)S(1)} %bitcast.173), kind=kCustom, calls=%fused_computation.37.clone.1 | custom fusion | flops 786432 | bytes 1056772 | tf_op jit(solution)/shard_map/while/body/eval_jaxpr/scatter-add | solution.py:180
  314.0 7.1 %scatter_custom_fusion.6 = f32[1024,256]{1,0:T(8,128)S(1)} fusion(f32[1024,256]{1,0:T(8,128)S(1)} %get-tuple-element.566, s32[1024]{0:T(1024)S(1)} %bitcast.177, f32[]{:T(128)} %constant.116.clone.1..sunk, f32[1024]{0:T(1024)S(1)} %bitcast.172, s32[1024]{0:T(1024)S(1)} %bitcast.173), kind=kCustom, calls=%fused_computation.37.clone.1 | custom fusion | flops 786432 | bytes 1056772 | tf_op jit(solution)/shard_map/while/body/eval_jaxpr/scatter-add | solution.py:180
  321.9 7.1 %scatter_custom_fusion.6 = f32[1024,256]{1,0:T(8,128)S(1)} fusion(f32[1024,256]{1,0:T(8,128)S(1)} %get-tuple-element.566, s32[1024]{0:T(1024)S(1)} %bitcast.177, f32[]{:T(128)} %constant.116.clone.1..sunk, f32[1024]{0:T(1024)S(1)} %bitcast.172, s32[1024]{0:T(1024)S(1)} %bitcast.173), kind=kCustom, calls=%fused_computation.37.clone.1 | custom fusion | flops 786432 | bytes 1056772 | tf_op jit(solution)/shard_map/while/body/eval_jaxpr/scatter-add | solution.py:180
  329.9 7.1 %scatter_custom_fusion.6 = f32[1024,256]{1,0:T(8,128)S(1)} fusion(f32[1024,256]{1,0:T(8,128)S(1)} %get-tuple-element.566, s32[1024]{0:T(1024)S(1)} %bitcast.177, f32[]{:T(128)} %constant.116.clone.1..sunk, f32[1024]{0:T(1024)S(1)} %bitcast.172, s32[1024]{0:T(1024)S(1)} %bitcast.173), kind=kCustom, calls=%fused_computation.37.clone.1 | custom fusion | flops 786432 | bytes 1056772 | tf_op jit(solution)/shard_map/while/body/eval_jaxpr/scatter-add | solution.py:180
  337.8 7.1 %scatter_custom_fusion.6 = f32[1024,256]{1,0:T(8,128)S(1)} fusion(f32[1024,256]{1,0:T(8,128)S(1)} %get-tuple-element.566, s32[1024]{0:T(1024)S(1)} %bitcast.177, f32[]{:T(128)} %constant.116.clone.1..sunk, f32[1024]{0:T(1024)S(1)} %bitcast.172, s32[1024]{0:T(1024)S(1)} %bitcast.173), kind=kCustom, calls=%fused_computation.37.clone.1 | custom fusion | flops 786432 | bytes 1056772 | tf_op jit(solution)/shard_map/while/body/eval_jaxpr/scatter-add | solution.py:180
  345.7 7.1 %scatter_custom_fusion.6 = f32[1024,256]{1,0:T(8,128)S(1)} fusion(f32[1024,256]{1,0:T(8,128)S(1)} %get-tuple-element.566, s32[1024]{0:T(1024)S(1)} %bitcast.177, f32[]{:T(128)} %constant.116.clone.1..sunk, f32[1024]{0:T(1024)S(1)} %bitcast.172, s32[1024]{0:T(1024)S(1)} %bitcast.173), kind=kCustom, calls=%fused_computation.37.clone.1 | custom fusion | flops 786432 | bytes 1056772 | tf_op jit(solution)/shard_map/while/body/eval_jaxpr/scatter-add | solution.py:180
  353.7 7.1 %scatter_custom_fusion.6 = f32[1024,256]{1,0:T(8,128)S(1)} fusion(f32[1024,256]{1,0:T(8,128)S(1)} %get-tuple-element.566, s32[1024]{0:T(1024)S(1)} %bitcast.177, f32[]{:T(128)} %constant.116.clone.1..sunk, f32[1024]{0:T(1024)S(1)} %bitcast.172, s32[1024]{0:T(1024)S(1)} %bitcast.173), kind=kCustom, calls=%fused_computation.37.clone.1 | custom fusion | flops 786432 | bytes 1056772 | tf_op jit(solution)/shard_map/while/body/eval_jaxpr/scatter-add | solution.py:180
  361.6 7.1 %scatter_custom_fusion.6 = f32[1024,256]{1,0:T(8,128)S(1)} fusion(f32[1024,256]{1,0:T(8,128)S(1)} %get-tuple-element.566, s32[1024]{0:T(1024)S(1)} %bitcast.177, f32[]{:T(128)} %constant.116.clone.1..sunk, f32[1024]{0:T(1024)S(1)} %bitcast.172, s32[1024]{0:T(1024)S(1)} %bitcast.173), kind=kCustom, calls=%fused_computation.37.clone.1 | custom fusion | flops 786432 | bytes 1056772 | tf_op jit(solution)/shard_map/while/body/eval_jaxpr/scatter-add | solution.py:180
  369.5 7.1 %scatter_custom_fusion.6 = f32[1024,256]{1,0:T(8,128)S(1)} fusion(f32[1024,256]{1,0:T(8,128)S(1)} %get-tuple-element.566, s32[1024]{0:T(1024)S(1)} %bitcast.177, f32[]{:T(128)} %constant.116.clone.1..sunk, f32[1024]{0:T(1024)S(1)} %bitcast.172, s32[1024]{0:T(1024)S(1)} %bitcast.173), kind=kCustom, calls=%fused_computation.37.clone.1 | custom fusion | flops 786432 | bytes 1056772 | tf_op jit(solution)/shard_map/while/body/eval_jaxpr/scatter-add | solution.py:180
  376.7 9.7 %all-to-all-start.2 = ((f32[16,1,1024]{2,1,0:T(1,128)}), f32[16,1,1024]{2,1,0:T(1,128)S(1)}, u32[]{:S(2)}, u32[]{:S(2)}) async-start(f32[16,1,1024]{2,1,0:T(1,128)} %all_to_all.40), calls=%async_computation.2 | async-start | bytes 131072 | tf_op jit(solution)/shard_map/all_to_all | solution.py:40
  386.4 1.8 copy.28
  393.0 2.0 multiply_subtract_fusion
  395.0 2.0 collective-permute-start.1
  399.9 4.2 %fusion.28 = f32[1,4,256,256]{3,2,1,0:T(8,128)} fusion(f32[4,256,256]{1,2,0:T(8,128)S(1)} %convolution_bitcast_fusion, f32[4,256,512]{2,1,0:T(8,128)} %bitcast.167, f32[4]{0:T(128)S(1)} %dynamic-slice_multiply_fusion, f32[256,256]{1,0:T(8,128)} %param.32, f32[1,4,256,256]{3,2,1,0:T(8,128)S(1)} %bitcast.159), kind=kOutput, calls=%fused_computation.68 | convolution fusion | flops 806092800 | bytes 4456464 | tf_op jit(solution)/shard_map/lxb,yb->lxy/dot_general | solution.py:100
  404.2 17.7 %collective-permute-done.1 = f32[4,256,256]{2,1,0:T(8,128)} collective-permute-done((f32[4,256,256]{2,1,0:T(8,128)}, f32[4,256,256]{2,1,0:T(8,128)}, u32[]{:S(2)}, u32[]{:S(2)}) %collective-permute-start.1) | collective-permute-done | bytes 1048608 | tf_op jit(solution)/shard_map/ppermute | solution.py:15
  421.9 2.4 add_bitcast_fusion
  (249 shorter events, 83.7 us)
Async XLA Ops:
  0.6 172.1 %copy-start = (f32[256,256]{1,0:T(8,128)S(1)}, f32[256,256]{1,0:T(8,128)}, u32[]{:S(2)}) copy-start(f32[256,256]{1,0:T(8,128)} %param.31) | copy-start | bytes 786436
  0.6 29.6 %collective-permute-start = (f32[4,256,256]{2,1,0:T(8,128)}, f32[4,256,256]{2,1,0:T(8,128)S(1)}, u32[]{:S(2)}, u32[]{:S(2)}) collective-permute-start(f32[4,256,256]{2,1,0:T(8,128)} %bitcast.157), channel_id=1, source_target_pairs={{0,16},{16,32},{32,48},{48,64},{64,80},{80,96},{96,112},{112,128},... | collective-permute-start | bytes 3145736 | tf_op jit(solution)/shard_map/ppermute | solution.py:15
  5.8 28.2 %copy-start.10 = (f32[4]{0:T(128)}, f32[4]{0:T(128)S(1)}, u32[]{:S(2)}) copy-start(f32[4]{0:T(128)S(1)} %dynamic_slice.63) | copy-start | bytes 52
  6.5 27.5 %copy-start.12 = (f32[4]{0:T(128)}, f32[4]{0:T(128)S(1)}, u32[]{:S(2)}) copy-start(f32[4]{0:T(128)S(1)} %dynamic_slice.64) | copy-start | bytes 52
  32.8 2.6 copy-start.4
  38.3 11.9 %copy-start.1 = (f32[1,4,256,256]{3,2,1,0:T(8,128)S(1)}, f32[1,4,256,256]{3,2,1,0:T(8,128)}, u32[]{:S(2)}) copy-start(f32[1,4,256,256]{3,2,1,0:T(8,128)} %param.21) | copy-start | bytes 3145732
  38.3 137.1 %all-to-all-start = ((f32[4,256,512]{2,0,1:T(4,128)}), f32[4,256,512]{2,0,1:T(4,128)}, u32[]{:S(2)}, u32[]{:S(2)}) async-start(f32[4,256,512]{2,0,1:T(4,128)} %copy.26), calls=%async_computation | async-start | bytes 4194304 | tf_op jit(solution)/shard_map/all_to_all | solution.py:26
  50.3 87.0 %copy-start.14 = (f32[1,1024]{1,0:T(1,128)S(1)}, f32[1,1024]{1,0:T(1,128)}, u32[]{:S(2)}) copy-start(f32[1,1024]{1,0:T(1,128)} %param.23) | copy-start | bytes 12292
  179.4 2.2 copy-start.2
  179.4 2.2 copy-start.3
  179.4 2.2 copy-start.17
  245.3 131.4 %all-to-all-start.1 = ((f32[64,16,512]{2,1,0:T(8,128)}), f32[64,16,512]{2,1,0:T(8,128)}, u32[]{:S(2)}, u32[]{:S(2)}) async-start(f32[64,16,512]{2,1,0:T(8,128)} %pad_maximum_fusion.1), calls=%async_computation.1 | async-start | bytes 4194304 | tf_op jit(solution)/shard_map/all_to_all | solution.py:26
  376.7 11.6 %copy-start.7 = (f32[1024,256]{1,0:T(8,128)}, f32[1024,256]{1,0:T(8,128)S(1)}, u32[]{:S(2)}) copy-start(f32[1024,256]{1,0:T(8,128)S(1)} %get-tuple-element.302) | copy-start | bytes 3145732
  376.7 22.6 %all-to-all-start.2 = ((f32[16,1,1024]{2,1,0:T(1,128)}), f32[16,1,1024]{2,1,0:T(1,128)S(1)}, u32[]{:S(2)}, u32[]{:S(2)}) async-start(f32[16,1,1024]{2,1,0:T(1,128)} %all_to_all.40), calls=%async_computation.2 | async-start | bytes 131072 | tf_op jit(solution)/shard_map/all_to_all | solution.py:40
  388.2 1.3 copy-start.5
  388.2 1.4 copy-start.11
  388.3 1.4 copy-start.13
  391.9 5.1 %copy-start.6 = (f32[4,256,256]{1,2,0:T(8,128)S(1)}, f32[4,256,256]{1,2,0:T(8,128)}, u32[]{:S(2)}) copy-start(f32[4,256,256]{1,2,0:T(8,128)} %convolution_bitcast_fusion.1) | copy-start | bytes 3145732
  391.9 5.1 %copy-start.9 = (f32[256,256]{1,0:T(8,128)S(1)}, f32[256,256]{1,0:T(8,128)}, u32[]{:S(2)}) copy-start(f32[256,256]{1,0:T(8,128)} %param.32) | copy-start | bytes 786436
  395.0 4.2 copy-start.18
  395.0 4.4 %copy-start.15 = (f32[1,1024]{1,0:T(1,128)S(1)}, f32[1,1024]{1,0:T(1,128)}, u32[]{:S(2)}) copy-start(f32[1,1024]{1,0:T(1,128)} %param.23) | copy-start | bytes 12292
  395.0 4.4 %copy-start.16 = (f32[1,1024]{1,0:T(1,128)S(1)}, f32[1,1024]{1,0:T(1,128)}, u32[]{:S(2)}) copy-start(f32[1,1024]{1,0:T(1,128)} %param.25) | copy-start | bytes 12292
  395.0 26.9 %collective-permute-start.1 = (f32[4,256,256]{2,1,0:T(8,128)}, f32[4,256,256]{2,1,0:T(8,128)}, u32[]{:S(2)}, u32[]{:S(2)}) collective-permute-start(f32[4,256,256]{2,1,0:T(8,128)} %multiply_subtract_fusion), channel_id=1, source_target_pairs={{16,0},{32,16},{48,32},{64,48},{80,64},{96,80},{112,96},{128,112},... | collective-permute-start | bytes 3145736 | tf_op jit(solution)/shard_map/ppermute | solution.py:15
  399.9 22.0 %copy-start.8 = (f32[1024,256]{1,0:T(8,128)S(1)}, f32[1024,256]{1,0:T(8,128)}, u32[]{:S(2)}) copy-start(f32[1024,256]{1,0:T(8,128)} %copy-done.7) | copy-start | bytes 3145732
where the time goes:
time: 428 us; the launch traced here: 424 us
  other arithmetic  141 us (33%)
  local copies, waits for them, and re-layouts  125 us (29%)
  matrix products  51.6 us (12%)
  waiting for transfers between devices  40.1 us (9%)
  blocking collectives  31.9 us (7%)
  starting transfers between devices  31.7 us (7%)
    scatter-add x16, other arithmetic, add_block(): return total.at[block_rows_index].add(spread_rows, mode='drop')  114 us
    gather x16, local copies, waits for them, and re-layouts, pick_block(): jnp.take(flat_state, block_rows_index, axis=0, mode='fill', fill_value=0.0)  55.4 us
    ppermute x2, waiting for transfers between devices, from_behind(): lax.ppermute(value, axis, [(source, source + steps) for source in range(f...  40.1 us
    all_gather x1, blocking collectives, body(): duals = lax.all_gather(obs_dual[0], 'space', axis=0, tiled=True)  31.9 us
    dynamic_update_slice x16, local copies, waits for them, and re-layouts, body(): seen = lax.map(pick_block, (index_blocks, column_blocks)).reshape(-1)  22.4 us
    all_to_all x2, starting transfers between devices, side_by_side(): lax.all_to_all(both, axis, split_axis=split_dim, concat_axis=concat_dim,...  16.3 us
    dot_general x4, matrix products, visit(): jnp.dot(layer_in, path, preferred_element_type=jnp.float32)  14.6 us
    dot_general x4, matrix products, visit(): jnp.dot(layer_in.T, back_hidden, preferred_element_type=jnp.float32)  13.9 us
  transfers between devices with their start and end apart: 5, of which 2 were waited for; matrix products, arithmetic and copies ran while one was open for 55% of the time, Pallas kernels for 0%

commit v1 on v0

v1 whole, which is shorter than its diff:
```python
import jax
import jax.numpy as jnp
from jax import lax
from jax.experimental import pallas as pl
from jax.experimental.pallas import tpu as pltpu
from jax.sharding import PartitionSpec as P

STEPS = 4
MESH = pl.DeviceIdType.MESH
F32, BF16 = jnp.float32, jnp.bfloat16
PARTNERS = (8, 12, 10, 14, 9, 13, 11, 15, 4, 6, 2, 5, 7, 3, 1)
BLOCK = 512
LANES = 128


def flip(value, mask):
    for bit in (1, 2, 4, 8):
        if mask & bit:
            value = value + bit * (1 - 2 * lax.rem(lax.div(value, bit), 2))
    return value


def split_two(value):
    high = value.astype(BF16)
    low = (value - high.astype(F32)).astype(BF16)
    return high, low


def dot(a, b):
    return jnp.dot(a, b, preferred_element_type=F32)


def dot_nt(a, b, precision=None):
    return lax.dot_general(
        a, b, (((1,), (1,)), ((), ())), precision=precision, preferred_element_type=F32
    )


def dot_three(a, b):
    return dot(a[0], b[0]) + (dot(a[0], b[1]) + dot(a[1], b[0]))


def stencil(field, diffusion, drift_rows, drift_cols, direction):
    rows, cols = field.shape
    row_id = lax.broadcasted_iota(jnp.int32, field.shape, 0)
    col_id = lax.broadcasted_iota(jnp.int32, field.shape, 1)
    centre = 1.0 - 4.0 * diffusion
    row_up, row_dn = diffusion - direction * drift_rows, diffusion + direction * drift_rows
    col_up, col_dn = diffusion - direction * drift_cols, diffusion + direction * drift_cols
    for _ in range(STEPS):
        up1 = jnp.where(row_id == rows - 1, 0.0, pltpu.roll(field, rows - 1, 0))
        dn1 = jnp.where(row_id == 0, 0.0, pltpu.roll(field, 1, 0))
        up2 = jnp.where(col_id == cols - 1, 0.0, pltpu.roll(field, cols - 1, 1))
        dn2 = jnp.where(col_id == 0, 0.0, pltpu.roll(field, 1, 1))
        field = centre * field + (row_up * up1 + row_dn * dn1) + (col_up * up2 + col_dn * dn2)
    return field


def kernel(
    sites, dual, variance, diffusion, drift_rows, drift_cols, spread, row_factor, col_factor,
    w_in, bias, w_out, inc_any, mult_any, traj_any,
    state_any, obs_out, mult_out_any,
    inc, mult, stepped, traj, path, strip_m, strip_i, slopes, out_b, out_f, slab_b, slab_f,
    before, placed, picked, w_path, w_tangent, w_adjoint, w_in_t, duals, seen, seen_in,
    outs, outm,
    load_sem, store_sem, m_send, m_recv, i_send, i_recv, b_send, b_recv, f_send, f_recv,
    d_send, d_recv, s_send, s_recv, keep_sem,
):
    depth, rows, cols = inc.shape
    chunks, levels, strip, _ = strip_m.shape
    hidden = w_in.shape[0]
    spaces = rows // strip
    w, s = lax.axis_index("win"), lax.axis_index("space")
    wins = lax.axis_size("win")
    after, prior = lax.rem(w + 1, wins), lax.rem(w + wins - 1, wins)
    first = s * depth

    barrier = pltpu.get_barrier_semaphore()
    for p in range(spaces):
        d = flip(s, p)
        for win in (w, after, prior):
            if win is w and p == 0:
                continue
            pl.semaphore_signal(
                barrier, inc=1, device_id={"win": win, "space": d}, device_id_type=MESH
            )

    load_inc = pltpu.make_async_copy(inc_any, inc, load_sem.at[0])
    load_traj = pltpu.make_async_copy(traj_any, traj, load_sem.at[1])
    load_mult = pltpu.make_async_copy(mult_any, mult, load_sem.at[2])
    load_inc.start()
    load_traj.start()
    load_mult.start()

    lane = lax.broadcasted_iota(jnp.int32, (hidden, 2 * levels), 1)
    bias_all = jnp.broadcast_to(bias[...], (2 * levels, hidden)).T
    bias_hi = bias_all.astype(BF16).astype(F32)
    bias_mid = (bias_all - bias_hi).astype(BF16).astype(F32)
    bias_lo = bias_all - bias_hi - bias_mid
    w_in32, w_out32 = w_in[...].astype(F32), w_out[...].astype(F32)
    wide = jnp.concatenate([w_in32, jnp.zeros((hidden, levels), F32)], 1)
    wide = jnp.where(lane == levels, bias_hi, wide)
    wide = jnp.where(lane == levels + 1, bias_mid, wide)
    wide = jnp.where(lane == levels + 2, bias_lo, wide)
    w_path[...] = (0.5 * wide).astype(BF16)
    w_tangent[...] = (0.5 * w_in32).astype(BF16)
    w_adjoint[...] = (0.5 * w_out32.T).astype(BF16)
    w_in_t[...] = w_in32.T.astype(BF16)

    load_inc.wait()

    def step_forward(level, carry):
        at = first + level
        stepped[level] = stencil(
            inc[level], diffusion[at], drift_rows[at], drift_cols[at], 1.0
        )
        return carry

    lax.fori_loop(0, depth, step_forward, 0)

    pl.semaphore_wait(barrier, 3 * spaces - 1)

    def remote(src, dst, send, recv, win, space):
        return pltpu.make_async_remote_copy(
            src_ref=src, dst_ref=dst, send_sem=send, recv_sem=recv,
            device_id={"win": win, "space": space}, device_id_type=MESH,
        )

    def strip_of(d):
        return pl.ds(pl.multiple_of(d * strip, strip), strip)

    def depth_of(d):
        return pl.ds(pl.multiple_of(d * depth, depth), depth)

    def chunk_of(c):
        return pl.ds(c * LANES, LANES)

    def dual_copy(p):
        return remote(dual, duals.at[pl.ds(2 * s, 2)], d_send.at[p], d_recv.at[p], w, flip(s, p))

    def mult_copy(p, c):
        d = flip(s, p)
        return remote(
            mult_any.at[:, strip_of(d), chunk_of(c)], strip_m.at[c, depth_of(s)],
            m_send.at[c, p], m_recv.at[c, p], w, d,
        )

    def inc_copy(p, c):
        d = flip(s, p)
        return remote(
            stepped.at[:, strip_of(d), chunk_of(c)], strip_i.at[c, depth_of(s)],
            i_send.at[c, p], i_recv.at[c, p], after, d,
        )

    def back_copy(p, c):
        d = flip(s, p)
        return remote(
            out_b.at[c, depth_of(d)], slab_b.at[:, strip_of(s), chunk_of(c)],
            b_send.at[c, p], b_recv.at[c, p], prior, d,
        )

    def ahead_copy(p, c):
        d = flip(s, p)
        return remote(
            out_f.at[c, depth_of(d)], slab_f.at[:, strip_of(s), chunk_of(c)],
            f_send.at[c, p], f_recv.at[c, p], w, d,
        )

    def seen_copy(p):
        d = flip(s, p)
        return remote(
            seen.at[pl.ds(2 * d, 2)], seen_in.at[s], s_send.at[p], s_recv.at[p], w, d
        )

    keep_dual = pltpu.make_async_copy(dual, duals.at[pl.ds(2 * s, 2)], keep_sem.at[0])
    keep_seen = pltpu.make_async_copy(seen.at[pl.ds(2 * s, 2)], seen_in.at[s], keep_sem.at[1])

    def keep_mult(c):
        return pltpu.make_async_copy(
            mult_any.at[:, strip_of(s), chunk_of(c)], strip_m.at[c, depth_of(s)],
            keep_sem.at[2 + c],
        )

    def keep_ahead(c):
        return pltpu.make_async_copy(
            out_f.at[c, depth_of(s)], slab_f.at[:, strip_of(s), chunk_of(c)],
            keep_sem.at[2 + chunks + c],
        )

    everyone = PARTNERS + (0,)
    has_prior, has_after = w > 0, w < wins - 1

    keep_dual.start()
    for p in PARTNERS:
        dual_copy(p).start()

    @pl.when(has_prior)
    def _():
        for c in range(chunks):
            for p in PARTNERS:
                mult_copy(p, c).start()
            keep_mult(c).start()

    @pl.when(has_after)
    def _():
        for c in range(chunks):
            for p in everyone:
                inc_copy(p, c).start()

    load_traj.wait()
    for c in range(chunks):
        path[c] = traj[:, :, c * LANES : (c + 1) * LANES].astype(F32).reshape(levels * strip, LANES)
    ones = jnp.ones((levels, 2 * LANES), F32)
    flat = (chunks * levels * strip, LANES)

    def two_rows(ref, c, pair):
        at = c * levels * strip + 2 * pair
        return jnp.concatenate(
            [ref[pl.ds(at + k, levels, stride=strip), :] for k in range(2)], 1
        )

    def slope_rows(at, carry):
        c, pair = lax.div(at, strip // 2), lax.rem(at, strip // 2)
        line = jnp.concatenate([two_rows(path.reshape(flat), c, pair), ones], 0).astype(BF16)
        for m in range(4):
            part = slice(m * hidden // 4, (m + 1) * hidden // 4)
            half_act = dot(w_path[part, :], line)
            bend = jnp.tanh(half_act)
            slopes[at, part, :] = (1.0 + bend) * (1.0 + half_act * (1.0 - bend))
        return carry

    lax.fori_loop(0, chunks * strip // 2, slope_rows, 0)

    def network(source, target, w_first, w_second):
        def visit(at, carry):
            c, pair = lax.div(at, strip // 2), lax.rem(at, strip // 2)
            line = two_rows(source.reshape(flat), c, pair)
            narrow = line.astype(BF16)
            parts = []
            for m in range(4):
                part = slice(m * hidden // 4, (m + 1) * hidden // 4)
                parts.append((slopes[at, part, :] * dot(w_first[part, :], narrow)).astype(BF16))
            line = line + dot(w_second[...], jnp.concatenate(parts, 0))
            for k in range(2):
                row = c * levels * strip + 2 * pair + k
                target.reshape(flat)[pl.ds(row, levels, stride=strip), :] = line[
                    :, k * LANES : (k + 1) * LANES
                ]
            return carry

        return visit

    load_mult.wait()
    exact = lax.Precision.HIGHEST
    left = split_two(dot_nt(row_factor[...], row_factor[...], exact))
    right = split_two(dot_nt(col_factor[...], col_factor[...], exact))

    def correlate(level, carry):
        scale = spread[first + level]
        inner = split_two(dot_three(left, split_two(mult[level])))
        before[level] = (scale * scale) * dot_three(inner, right) + inc[level]
        return carry

    lax.fori_loop(0, depth, correlate, 0)

    for level in range(depth):
        high, low = split_two(inc[level].T)
        part = slice(level * rows, (level + 1) * rows)
        picked[0:cols, part] = high
        picked[cols : 2 * cols, part] = low
    placed[...] = jnp.zeros_like(placed)
    keep_dual.wait()
    for p in PARTNERS:
        dual_copy(p).wait_recv()
    row_ids = lax.broadcasted_iota(jnp.int32, (depth * rows, BLOCK), 0)
    col_ids = lax.broadcasted_iota(jnp.int32, (cols, BLOCK), 0)

    def observe(block, carry):
        here = pl.ds(pl.multiple_of(block * BLOCK, BLOCK), BLOCK)
        local = sites[0:1, here] - first
        inside = (local >= 0) & (local < depth)
        row_at = jnp.where(inside, local * rows + sites[1:2, here], -1)
        hot = jnp.where(row_ids == row_at, 1.0, 0.0).astype(BF16)
        chosen = col_ids == sites[2:3, here]
        value = duals[block]
        high = value.astype(BF16).astype(F32)
        low = value - high
        spots = jnp.concatenate(
            [jnp.where(chosen, high, 0.0).astype(BF16), jnp.where(chosen, low, 0.0).astype(BF16)], 1
        )
        placed[...] += dot_nt(jnp.concatenate([hot, hot], 1), spots)
        found = dot(picked[...], hot)
        found = found[0:cols] + found[cols : 2 * cols]
        seen[block] = jnp.sum(jnp.where(chosen, found, 0.0), axis=0, keepdims=True)
        return carry

    blocks = sites.shape[1] // BLOCK
    cut = blocks // 2

    adjoint = network(strip_m, out_b, w_adjoint, w_in_t)
    tangent = network(strip_i, out_f, w_tangent, w_out)

    @pl.when(has_prior)
    def _():
        for c in range(chunks):
            keep_mult(c).wait()
            for p in PARTNERS:
                mult_copy(p, c).wait_recv()
            lax.fori_loop(c * strip // 2, (c + 1) * strip // 2, adjoint, 0)
            for p in everyone:
                back_copy(p, c).start()

    lax.fori_loop(0, cut, observe, 0)

    @pl.when(has_prior)
    def _():
        for c in range(chunks):
            for p in everyone:
                inc_copy(p, c).wait_recv()
            lax.fori_loop(c * strip // 2, (c + 1) * strip // 2, tangent, 0)
            for p in PARTNERS:
                ahead_copy(p, c).start()
            keep_ahead(c).start()

    lax.fori_loop(cut, blocks, observe, 0)
    for p in PARTNERS:
        seen_copy(p).start()
    keep_seen.start()

    def add_placed(level):
        return mult[level] + placed[pl.ds(pl.multiple_of(level * rows, rows), rows), :]

    @pl.when(has_after)
    def _():
        for c in range(chunks):
            for p in everyone:
                back_copy(p, c).wait_recv()

        def step_back(level, carry):
            at = first + level
            later = stencil(slab_b[level], diffusion[at], drift_rows[at], drift_cols[at], -1.0)
            outm[level] = add_placed(level) - later
            return carry

        lax.fori_loop(0, depth, step_back, 0)

    @pl.when(w == wins - 1)
    def _():
        def plain(level, carry):
            outm[level] = add_placed(level)
            return carry

        lax.fori_loop(0, depth, plain, 0)

    store_mult = pltpu.make_async_copy(outm, mult_out_any, store_sem.at[0])
    store_mult.start()

    keep_seen.wait()
    for p in PARTNERS:
        seen_copy(p).wait_recv()
    obs_out[...] = variance[...] * dual[...] + jnp.sum(seen_in[...], axis=0)

    @pl.when(has_prior)
    def _():
        for c in range(chunks):
            keep_ahead(c).wait()
            for p in PARTNERS:
                ahead_copy(p, c).wait_recv()

        def subtract(level, carry):
            outs[level] = before[level] - slab_f[level]
            return carry

        lax.fori_loop(0, depth, subtract, 0)

    @pl.when(w == 0)
    def _():
        outs[...] = before[...]

    store_state = pltpu.make_async_copy(outs, state_any, store_sem.at[1])
    store_state.start()

    for p in PARTNERS:
        dual_copy(p).wait_send()
        seen_copy(p).wait_send()

    @pl.when(has_prior)
    def _():
        for c in range(chunks):
            for p in everyone:
                back_copy(p, c).wait_send()
            for p in PARTNERS:
                mult_copy(p, c).wait_send()
                ahead_copy(p, c).wait_send()

    @pl.when(has_after)
    def _():
        for c in range(chunks):
            for p in everyone:
                inc_copy(p, c).wait_send()

    store_mult.wait()
    store_state.wait()


def body(
    increment, multiplier, obs_dual, obs_sites, obs_variance, trajectory, diffusion, drift_rows,
    drift_cols, spread, row_factor, col_factor, layer_in, bias_in, layer_out,
):
    _, depth, rows, cols = increment.shape
    _, levels, strip, _ = trajectory.shape
    hidden = layer_in.shape[0]
    own = obs_dual.shape[1]
    spaces = lax.axis_size("space")
    pair = (own // BLOCK, 1, BLOCK)
    slab = pltpu.VMEM((depth, rows, cols), F32)
    chunks = cols // LANES
    row_strip = pltpu.VMEM((chunks, levels, strip, LANES), F32)
    vmem = pl.BlockSpec(memory_space=pltpu.VMEM)
    smem = pl.BlockSpec(memory_space=pltpu.SMEM)
    anywhere = pl.BlockSpec(memory_space=pl.ANY)
    dma = pltpu.SemaphoreType.DMA
    state, seen, mult_out = pl.pallas_call(
        kernel,
        out_shape=(
            jax.ShapeDtypeStruct((depth, rows, cols), F32),
            jax.ShapeDtypeStruct(pair, F32),
            jax.ShapeDtypeStruct((depth, rows, cols), F32),
        ),
        in_specs=[vmem] * 3 + [smem] * 4 + [vmem] * 5 + [anywhere] * 3,
        out_specs=(anywhere, vmem, anywhere),
        scratch_shapes=[
            slab, slab, slab,
            pltpu.VMEM((levels, strip, cols), BF16),
            pltpu.VMEM((chunks, levels * strip, LANES), F32),
            row_strip, row_strip,
            pltpu.VMEM((chunks * strip // 2, hidden, 2 * LANES), F32),
            row_strip, row_strip,
            slab, slab, slab,
            pltpu.VMEM((depth * rows, cols), F32),
            pltpu.VMEM((2 * cols, depth * rows), BF16),
            pltpu.VMEM((hidden, 2 * levels), BF16),
            pltpu.VMEM((hidden, levels), BF16),
            pltpu.VMEM((hidden, levels), BF16),
            pltpu.VMEM((levels, hidden), BF16),
            pltpu.VMEM((spaces * own // BLOCK, 1, BLOCK), F32),
            pltpu.VMEM((spaces * own // BLOCK, 1, BLOCK), F32),
            pltpu.VMEM((spaces,) + pair, F32),
            slab, slab,
            dma((3,)), dma((2,)),
            *[dma((chunks, spaces))] * 8,
            *[dma((spaces,))] * 4,
            dma((2 + 2 * chunks,)),
        ],
        compiler_params=pltpu.CompilerParams(
            collective_id=0, has_side_effects=True, vmem_limit_bytes=60 * 1024 * 1024
        ),
        name="saddle",
    )(
        obs_sites[0], obs_dual.reshape(pair), obs_variance.reshape(pair),
        diffusion, drift_rows, drift_cols, spread, row_factor, col_factor,
        layer_in, bias_in.reshape(1, hidden), layer_out,
        increment[0], multiplier[0], trajectory[0],
    )
    return state[None], seen.reshape(1, own), mult_out[None]


def solution(mesh):
    placed = (
        P("win", "space", None, None), P("win", "space", None, None), P("win", "space"),
        P("win", None, None), P("win", "space"), P("win", None, "space", None),
        P(), P(), P(), P(), P(), P(), P(), P(), P(),
    )
    return jax.shard_map(
        body,
        mesh=mesh,
        in_specs=placed,
        out_specs=(P("win", "space", None, None), P("win", "space"), P("win", "space", None, None)),
        check_vma=False,
    )
```

time: 428 us -> 124 us (0.29)
  other arithmetic: 141 us -> 0 us
  local copies, waits for them, and re-layouts: 125 us -> 6.59 us
  Pallas kernels: 0 us -> 116 us
  matrix products: 51.6 us -> 0 us
  waiting for transfers between devices: 40.1 us -> 0 us
  blocking collectives: 31.9 us -> 0 us
  starting transfers between devices: 31.7 us -> 0 us
    pallas_call x0 -> x1, Pallas kernels: none -> 116 us  [body(): pl.pallas_call(kernel, out_shape=(jax.ShapeDtypeStruct((depth, rows, cols...]
    scatter-add x16 -> x0, other arithmetic: 114 us -> none  [add_block(): return total.at[block_rows_index].add(spread_rows, mode='drop')]
    gather x16 -> x0, local copies, waits for them, and re-layouts: 55.4 us -> none  [pick_block(): jnp.take(flat_state, block_rows_index, axis=0, mode='fill', fill_value=0.0)]
    dot_general x16 -> x0, matrix products: 51.6 us -> none  [the longest x4 14.6 us: visit(): jnp.dot(layer_in, path, preferred_element_type=jnp.float32)]
    ppermute x2 -> x0, waiting for transfers between devices: 40.1 us -> none  [from_behind(): lax.ppermute(value, axis, [(source, source + steps) for source in range(f...]
    all_gather x1 -> x0, blocking collectives: 31.9 us -> none  [body(): duals = lax.all_gather(obs_dual[0], 'space', axis=0, tiled=True)]
    dynamic_slice x63 -> x0, local copies, waits for them, and re-layouts: 27.7 us -> none  [the longest x12 12.8 us: select(): piece = lax.dynamic_slice_in_dim(source, first_row, block_rows, 1)]
    all_to_all x3 -> x0, starting transfers between devices: 26 us -> none  [the longest x2 16.3 us: side_by_side(): lax.all_to_all(both, axis, split_axis=split_dim, concat_axis=concat_dim,...]
  transfers between devices with their start and end apart: 5 -> 0, of which waited for: 2 -> 0; matrix products, arithmetic and copies ran while one was open for 55% -> 0% of each run, Pallas kernels for 0% -> 0%
where the time goes in v1:
time: 124 us; the launch traced here: 123 us
  Pallas kernels  116 us (94%)
  local copies, waits for them, and re-layouts  6.59 us (5%)
    pallas_call x1, Pallas kernels, body(): pl.pallas_call(kernel, out_shape=(jax.ShapeDtypeStruct((depth, rows, cols...  116 us
    unnamed x11, local copies, waits for them, and re-layouts  6.59 us

profile of v1, /device:TPU:25, one launch (start us, length us, event | category | flops | bytes accessed | tf_op | source)
XLA Modules:
  0.0 123.5 jit_solution(13509171165416918012)
XLA Ops:
  0.6 0.0 copy-start.1
  0.6 1.8 %copy.21 = s32[1,3,16384]{2,1,0:T(4,128)} copy(s32[1,3,16384]{2,0,1:T(1,128)} %param.18) | data formatting | bytes 393216
  2.4 0.0 copy-done.1
  2.4 0.8 copy.18.w_in
  3.3 116.2 %saddle.1 = (f32[4,256,256]{2,1,0:T(8,128)}, f32[2,1,512]{2,1,0:T(1,128)}, f32[4,256,256]{2,1,0:T(8,128)}) custom-call(s32[3,16384]{1,0:T(4,128)} %bitcast.12, f32[2,1,512]{2,1,0:T(1,128)} %bitcast.19, f32[2,1,512]{2,1,0:T(1,128)} %bitcast.20, f32[64]{0:T(128)} %diffusion.1, f32[64]{0:T(128)} %drift_rows.1, f32[64]{0:T(128)} %drift_cols.1, f32[64]{0:T(128)} %spread.1, ...), custom_call_target="tpu_custom_call" | custom-call | tf_op jit(solution)/shard_map/saddle/pallas_call | solution.py:423
  119.5 0.0 copy-start.2
  119.5 0.0 copy-start
  119.5 2.4 %copy.25 = f32[1,4,256,256]{3,2,1,0:T(8,128)} copy(f32[1,4,256,256]{3,2,1,0:T(8,128)} %bitcast.14) | data formatting | bytes 2097152
  121.9 0.0 copy-done.2
  121.9 0.6 copy.26
  122.5 0.0 copy-done
  122.5 1.0 copy.27
Async XLA Ops:
  0.6 1.8 %copy-start.1 = (bf16[1024,64]{0,1:T(8,128)(2,1)S(1)}, bf16[1024,64]{0,1:T(8,128)(2,1)}, u32[]{:S(2)}) copy-start(bf16[1024,64]{0,1:T(8,128)(2,1)} %param.27) | copy-start | bytes 393220
  119.5 2.4 %copy-start.2 = (f32[2,1,512]{2,1,0:T(1,128)S(1)}, f32[2,1,512]{2,1,0:T(1,128)}, u32[]{:S(2)}) copy-start(f32[2,1,512]{2,1,0:T(1,128)} %get-tuple-element.7) | copy-start | bytes 12292
  119.5 3.0 %copy-start = (f32[4,256,256]{2,1,0:T(8,128)S(1)}, f32[4,256,256]{2,1,0:T(8,128)}, u32[]{:S(2)}) copy-start(f32[4,256,256]{2,1,0:T(8,128)} %get-tuple-element.8) | copy-start | bytes 3145732

commit v2 on v1

v2 whole, which is shorter than its diff:
```python
import jax
import jax.numpy as jnp
from jax import lax
from jax.experimental import pallas as pl
from jax.experimental.pallas import tpu as pltpu
from jax.sharding import PartitionSpec as P

STEPS = 4
MESH = pl.DeviceIdType.MESH
F32, BF16 = jnp.float32, jnp.bfloat16
PARTNERS = (8, 12, 10, 14, 9, 13, 11, 15, 4, 6, 2, 5, 7, 3, 1)
BLOCK = 512
LANES = 128
VMEM_LIMIT = 44 * 1024 * 1024


def flip(value, mask):
    for bit in (1, 2, 4, 8):
        if mask & bit:
            value = value + bit * (1 - 2 * lax.rem(lax.div(value, bit), 2))
    return value


def split_two(value):
    high = value.astype(BF16)
    low = (value - high.astype(F32)).astype(BF16)
    return high, low


def dot(a, b):
    return jnp.dot(a, b, preferred_element_type=F32)


def dot_nt(a, b, precision=None):
    return lax.dot_general(
        a, b, (((1,), (1,)), ((), ())), precision=precision, preferred_element_type=F32
    )


def dot_three(a, b):
    return dot(a[0], b[0]) + (dot(a[0], b[1]) + dot(a[1], b[0]))


def stencil(field, diffusion, drift_rows, drift_cols, direction):
    rows, cols = field.shape
    edge = 8
    row_id = lax.broadcasted_iota(jnp.int32, (edge, cols), 0)
    col_id = lax.broadcasted_iota(jnp.int32, (1, cols), 1)
    centre = 1.0 - 4.0 * diffusion
    row_up, row_dn = diffusion - direction * drift_rows, diffusion + direction * drift_rows
    col_up = jnp.where(col_id == cols - 1, 0.0, diffusion - direction * drift_cols)
    col_dn = jnp.where(col_id == 0, 0.0, diffusion + direction * drift_cols)
    for _ in range(STEPS):
        up1 = pltpu.roll(field, rows - 1, 0)
        last = jnp.where(row_id == edge - 1, 0.0, up1[rows - edge :])
        up1 = jnp.concatenate([up1[: rows - edge], last], 0)
        dn1 = pltpu.roll(field, 1, 0)
        dn1 = jnp.concatenate([jnp.where(row_id == 0, 0.0, dn1[:edge]), dn1[edge:]], 0)
        up2 = pltpu.roll(field, cols - 1, 1)
        dn2 = pltpu.roll(field, 1, 1)
        field = centre * field + (row_up * up1 + row_dn * dn1) + (col_up * up2 + col_dn * dn2)
    return field


def kernel(
    sites_any, dual_any, variance_any, diffusion_any, drift_rows_any, drift_cols_any, spread_any,
    row_any, col_any, w_in_t_any, bias_any, w_out_any, inc_any, mult_any, traj_any,
    before_any, slab_f, obs_any, mult_out_any,
    sites, dual, variance, diffusion, drift_rows, drift_cols, spread, row_factor, col_factor,
    w_in_t, bias, w_out, inc, mult, traj,
    stepped, path, strip_m, strip_i, slopes, out_b, out_f, slab_b,
    before, placed, picked, w_path, w_tangent, w_adjoint, duals, seen, seen_in, outm, obs,
    load_sem, store_sem, m_send, m_recv, i_send, i_recv, b_send, b_recv, f_send, f_recv,
    d_send, d_recv, s_send, s_recv, keep_sem, level_sem,
):
    depth, rows, cols = inc.shape
    chunks, levels, strip, _ = strip_m.shape
    hidden = w_out.shape[1]
    spaces = rows // strip
    w, s = lax.axis_index("win"), lax.axis_index("space")
    wins = lax.axis_size("win")
    after, prior = lax.rem(w + 1, wins), lax.rem(w + wins - 1, wins)
    first = s * depth

    barrier = pltpu.get_barrier_semaphore()
    for p in PARTNERS + (0,):
        d = flip(s, p)
        for win in (w, after, prior):
            if win is w and p == 0:
                continue
            pl.semaphore_signal(
                barrier, inc=1, device_id={"win": win, "space": d}, device_id_type=MESH
            )

    loads = [
        pltpu.make_async_copy(src, dst, load_sem.at[k])
        for k, (src, dst) in enumerate((
            (inc_any, inc), (diffusion_any, diffusion), (drift_rows_any, drift_rows),
            (drift_cols_any, drift_cols), (w_in_t_any, w_in_t), (bias_any, bias),
            (w_out_any, w_out), (traj_any, traj), (mult_any, mult), (spread_any, spread),
            (row_any, row_factor), (col_any, col_factor), (sites_any, sites), (dual_any, dual),
            (variance_any, variance),
        ))
    ]
    for load in loads:
        load.start()
    pl.semaphore_wait(barrier, 3 * spaces - 1)

    def remote(src, dst, send, recv, win, space):
        return pltpu.make_async_remote_copy(
            src_ref=src, dst_ref=dst, send_sem=send, recv_sem=recv,
            device_id={"win": win, "space": space}, device_id_type=MESH,
        )

    def strip_of(d):
        return pl.ds(pl.multiple_of(d * strip, strip), strip)

    def depth_of(d):
        return pl.ds(pl.multiple_of(d * depth, depth), depth)

    def chunk_of(c):
        return pl.ds(c * LANES, LANES)

    def dual_copy(p):
        return remote(dual_any, duals.at[pl.ds(2 * s, 2)], d_send, d_recv, w, flip(s, p))

    def mult_copy(p, c):
        d = flip(s, p)
        return remote(
            mult_any.at[:, strip_of(d), chunk_of(c)], strip_m.at[c, depth_of(s)],
            m_send.at[c], m_recv.at[c], w, d,
        )

    def inc_copy(p, c):
        d = flip(s, p)
        return remote(
            stepped.at[:, strip_of(d), chunk_of(c)], strip_i.at[c, depth_of(s)],
            i_send.at[c], i_recv.at[c], after, d,
        )

    def back_copy(p, c):
        d = flip(s, p)
        return remote(
            out_b.at[c, depth_of(d)], slab_b.at[:, strip_of(s), chunk_of(c)],
            b_send.at[c], b_recv.at[c], prior, d,
        )

    def ahead_copy(p, c):
        d = flip(s, p)
        return remote(
            out_f.at[c, depth_of(d)], slab_f.at[:, strip_of(s), chunk_of(c)],
            f_send.at[c], f_recv.at[c], w, d,
        )

    def seen_copy(p):
        d = flip(s, p)
        return remote(
            seen.at[pl.ds(2 * d, 2)], seen_in.at[s], s_send, s_recv, w, d
        )

    keep_dual = pltpu.make_async_copy(dual_any, duals.at[pl.ds(2 * s, 2)], keep_sem.at[0])
    keep_seen = pltpu.make_async_copy(seen.at[pl.ds(2 * s, 2)], seen_in.at[s], keep_sem.at[1])

    def keep_mult(c):
        return pltpu.make_async_copy(
            mult_any.at[:, strip_of(s), chunk_of(c)], strip_m.at[c, depth_of(s)],
            keep_sem.at[2 + c],
        )

    def keep_ahead(c):
        return pltpu.make_async_copy(
            out_f.at[c, depth_of(s)], slab_f.at[:, strip_of(s), chunk_of(c)],
            keep_sem.at[2 + chunks + c],
        )

    others = spaces - 1

    def all_of(ref, send, recv):
        return remote(ref, ref, send, recv, w, s)

    def all_mult(c):
        return all_of(strip_m.at[c, pl.ds(0, others * depth)], m_send.at[c], m_recv.at[c])

    def all_inc(c):
        return all_of(strip_i.at[c], i_send.at[c], i_recv.at[c])

    def all_back(c):
        return all_of(out_b.at[c], b_send.at[c], b_recv.at[c])

    def all_ahead(c):
        return all_of(out_f.at[c, pl.ds(0, others * depth)], f_send.at[c], f_recv.at[c])

    all_dual = all_of(duals.at[pl.ds(0, others * 2)], d_send, d_recv)
    all_seen = all_of(seen.at[pl.ds(0, others * 2)], s_send, s_recv)
    everyone = PARTNERS + (0,)
    has_prior, has_after = w > 0, w < wins - 1

    keep_dual.start()
    for p in PARTNERS:
        dual_copy(p).start()

    @pl.when(has_prior)
    def _():
        for c in range(chunks):
            for p in PARTNERS:
                mult_copy(p, c).start()
            keep_mult(c).start()

    for load in loads[0:4]:
        load.wait()

    def step_forward(level, carry):
        at = first + level
        stepped[level] = stencil(
            inc[level], diffusion[at], drift_rows[at], drift_cols[at], 1.0
        )
        return carry

    lax.fori_loop(0, depth, step_forward, 0)

    @pl.when(has_after)
    def _():
        for c in range(chunks):
            for p in everyone:
                inc_copy(p, c).start()

    for load in loads[4:8]:
        load.wait()
    lane = lax.broadcasted_iota(jnp.int32, (hidden, 2 * levels), 1)
    bias_all = jnp.broadcast_to(bias[...], (2 * levels, hidden)).T
    bias_hi = bias_all.astype(BF16).astype(F32)
    bias_mid = (bias_all - bias_hi).astype(BF16).astype(F32)
    bias_lo = bias_all - bias_hi - bias_mid
    w_in32 = w_in_t[...].astype(F32).T
    wide = jnp.concatenate([w_in32, jnp.zeros((hidden, levels), F32)], 1)
    wide = jnp.where(lane == levels, bias_hi, wide)
    wide = jnp.where(lane == levels + 1, bias_mid, wide)
    wide = jnp.where(lane == levels + 2, bias_lo, wide)
    w_path[...] = (0.5 * wide).astype(BF16)
    w_tangent[...] = (0.5 * w_in32).astype(BF16)
    w_adjoint[...] = (0.5 * w_out[...].astype(F32).T).astype(BF16)

    for c in range(chunks):
        path[c] = traj[:, :, c * LANES : (c + 1) * LANES].astype(F32).reshape(levels * strip, LANES)
    ones = jnp.ones((levels, 2 * LANES), F32)
    flat = (chunks * levels * strip, LANES)

    def two_rows(ref, c, pair):
        at = c * levels * strip + 2 * pair
        return jnp.concatenate(
            [ref[pl.ds(at + k, levels, stride=strip), :] for k in range(2)], 1
        )

    def slope_rows(at, carry):
        c, pair = lax.div(at, strip // 2), lax.rem(at, strip // 2)
        line = jnp.concatenate([two_rows(path.reshape(flat), c, pair), ones], 0).astype(BF16)
        for m in range(4):
            part = slice(m * hidden // 4, (m + 1) * hidden // 4)
            half_act = dot(w_path[part, :], line)
            bend = jnp.tanh(half_act)
            slopes[at, part, :] = (1.0 + bend) * (1.0 + half_act * (1.0 - bend))
        return carry

    lax.fori_loop(0, chunks * strip // 2, slope_rows, 0)

    def network(source, target, w_first, w_second):
        def visit(at, carry):
            c, pair = lax.div(at, strip // 2), lax.rem(at, strip // 2)
            line = two_rows(source.reshape(flat), c, pair)
            narrow = line.astype(BF16)
            parts = []
            for m in range(4):
                part = slice(m * hidden // 4, (m + 1) * hidden // 4)
                parts.append((slopes[at, part, :] * dot(w_first[part, :], narrow)).astype(BF16))
            line = line + dot(w_second[...], jnp.concatenate(parts, 0))
            for k in range(2):
                row = c * levels * strip + 2 * pair + k
                target.reshape(flat)[pl.ds(row, levels, stride=strip), :] = line[
                    :, k * LANES : (k + 1) * LANES
                ]
            return carry

        return visit

    for load in loads[8:]:
        load.wait()
    exact = lax.Precision.HIGHEST
    left = split_two(dot_nt(row_factor[...], row_factor[...], exact))
    right = split_two(dot_nt(col_factor[...], col_factor[...], exact))

    def correlate(level, carry):
        scale = spread[first + level]
        inner = split_two(dot_three(left, split_two(mult[level])))
        before[level] = (scale * scale) * dot_three(inner, right) + inc[level]
        return carry

    lax.fori_loop(0, depth, correlate, 0)
    store_before = pltpu.make_async_copy(before, before_any, store_sem.at[0])
    store_before.start()

    for level in range(depth):
        high, low = split_two(inc[level].T)
        part = slice(level * rows, (level + 1) * rows)
        picked[0:cols, part] = high
        picked[cols : 2 * cols, part] = low
    placed[...] = jnp.zeros_like(placed)
    keep_dual.wait()
    all_dual.wait_recv()
    row_ids = lax.broadcasted_iota(jnp.int32, (depth * rows, BLOCK), 0)
    col_ids = lax.broadcasted_iota(jnp.int32, (cols, BLOCK), 0)

    def observe(block, carry):
        here = pl.ds(pl.multiple_of(block * BLOCK, BLOCK), BLOCK)
        local = sites[0, :, here] - first
        inside = (local >= 0) & (local < depth)
        row_at = jnp.where(inside, local * rows + sites[1, :, here], -1)
        hot = jnp.where(row_ids == row_at, 1.0, 0.0).astype(BF16)
        chosen = col_ids == sites[2, :, here]
        value = duals[block]
        high = value.astype(BF16).astype(F32)
        low = value - high
        spots = jnp.concatenate(
            [jnp.where(chosen, high, 0.0).astype(BF16), jnp.where(chosen, low, 0.0).astype(BF16)], 1
        )
        placed[...] += dot_nt(jnp.concatenate([hot, hot], 1), spots)
        found = dot(picked[...], hot)
        found = found[0:cols] + found[cols : 2 * cols]
        seen[block] = jnp.sum(jnp.where(chosen, found, 0.0), axis=0, keepdims=True)
        return carry

    blocks = sites.shape[2] // BLOCK
    cuts = [blocks * k // 32 for k in (0, 4, 13, 20, 32)]

    adjoint = network(strip_m, out_b, w_adjoint, w_in_t)
    tangent = network(strip_i, out_f, w_tangent, w_out)

    for c in range(chunks):

        @pl.when(has_prior)
        def _():
            keep_mult(c).wait()
            all_mult(c).wait_recv()
            lax.fori_loop(c * strip // 2, (c + 1) * strip // 2, adjoint, 0)
            for p in everyone:
                back_copy(p, c).start()

        lax.fori_loop(cuts[c], cuts[c + 1], observe, 0)

    for c in range(chunks):

        @pl.when(has_prior)
        def _():
            all_inc(c).wait_recv()
            lax.fori_loop(c * strip // 2, (c + 1) * strip // 2, tangent, 0)
            for p in PARTNERS:
                ahead_copy(p, c).start()
            keep_ahead(c).start()

        lax.fori_loop(cuts[2 + c], cuts[3 + c], observe, 0)

    def store_mult(level):
        return pltpu.make_async_copy(outm.at[level], mult_out_any.at[level], level_sem.at[level])

    for p in PARTNERS:
        seen_copy(p).start()
    keep_seen.start()

    def add_placed(level):
        return mult[level] + placed[pl.ds(pl.multiple_of(level * rows, rows), rows), :]


    @pl.when(has_after)
    def _():
        for c in range(chunks):
            all_back(c).wait_recv()

        def step_back(level, carry):
            at = first + level
            later = stencil(slab_b[level], diffusion[at], drift_rows[at], drift_cols[at], -1.0)
            outm[level] = add_placed(level) - later
            store_mult(level).start()
            return carry

        lax.fori_loop(0, depth, step_back, 0)

    @pl.when(w == wins - 1)
    def _():
        def plain(level, carry):
            outm[level] = add_placed(level)
            store_mult(level).start()
            return carry

        lax.fori_loop(0, depth, plain, 0)

    keep_seen.wait()
    all_seen.wait_recv()
    obs[...] = variance[...] * dual[...] + jnp.sum(seen_in[...], axis=0)
    store_obs = pltpu.make_async_copy(obs, obs_any, store_sem.at[2])
    store_obs.start()

    all_dual.wait_send()
    all_seen.wait_send()
    store_before.wait()

    @pl.when(has_after)
    def _():
        for c in range(chunks):
            all_inc(c).wait_send()

    @pl.when(has_prior)
    def _():
        for c in range(chunks):
            all_back(c).wait_send()
            all_mult(c).wait_send()

    for level in range(depth):
        store_mult(level).wait()
    store_obs.wait()

    @pl.when(has_prior)
    def _():
        for c in range(chunks):
            keep_ahead(c).wait()
            all_ahead(c).wait_recv()
        for c in range(chunks):
            all_ahead(c).wait_send()

    @pl.when(w == 0)
    def _():
        stepped[...] = jnp.zeros_like(stepped)
        blank = pltpu.make_async_copy(stepped, slab_f, store_sem.at[3])
        blank.start()
        blank.wait()


def body(
    increment, multiplier, obs_dual, obs_sites, obs_variance, trajectory, diffusion, drift_rows,
    drift_cols, spread, row_factor, col_factor, layer_in, bias_in, layer_out,
):
    _, depth, rows, cols = increment.shape
    _, levels, strip, _ = trajectory.shape
    hidden = layer_in.shape[0]
    own = obs_dual.shape[1]
    spaces = lax.axis_size("space")
    pair = (own // BLOCK, 1, BLOCK)
    slab = pltpu.VMEM((depth, rows, cols), F32)
    chunks = cols // LANES
    row_strip = pltpu.VMEM((chunks, levels, strip, LANES), F32)
    anywhere = pl.BlockSpec(memory_space=pl.ANY)
    smem = pltpu.SMEM((levels,), F32)
    dma = pltpu.SemaphoreType.DMA
    full = jax.ShapeDtypeStruct((depth, rows, cols), F32)
    before, ahead, seen, mult_out = pl.pallas_call(
        kernel,
        out_shape=(full, full, jax.ShapeDtypeStruct(pair, F32), full),
        in_specs=[anywhere] * 15,
        out_specs=(anywhere,) * 4,
        scratch_shapes=[
            pltpu.VMEM((3, 1, spaces * own), jnp.int32),
            pltpu.VMEM(pair, F32), pltpu.VMEM(pair, F32),
            smem, smem, smem, smem,
            pltpu.VMEM((rows, rows), F32), pltpu.VMEM((cols, cols), F32),
            pltpu.VMEM((levels, hidden), BF16),
            pltpu.VMEM((1, hidden), F32),
            pltpu.VMEM((levels, hidden), BF16),
            slab, slab,
            pltpu.VMEM((levels, strip, cols), BF16),
            slab,
            pltpu.VMEM((chunks, levels * strip, LANES), F32),
            row_strip, row_strip,
            pltpu.VMEM((chunks * strip // 2, hidden, 2 * LANES), F32),
            row_strip, row_strip,
            slab,
            slab,
            pltpu.VMEM((depth * rows, cols), F32),
            pltpu.VMEM((2 * cols, depth * rows), BF16),
            pltpu.VMEM((hidden, 2 * levels), BF16),
            pltpu.VMEM((hidden, levels), BF16),
            pltpu.VMEM((hidden, levels), BF16),
            pltpu.VMEM((spaces * own // BLOCK, 1, BLOCK), F32),
            pltpu.VMEM((spaces * own // BLOCK, 1, BLOCK), F32),
            pltpu.VMEM((spaces,) + pair, F32),
            slab,
            pltpu.VMEM(pair, F32),
            dma((15,)), dma((4,)),
            *[dma((chunks,))] * 8,
            *[dma] * 4,
            dma((2 + 2 * chunks,)), dma((depth,)),
        ],
        compiler_params=pltpu.CompilerParams(
            collective_id=0, has_side_effects=True, vmem_limit_bytes=VMEM_LIMIT
        ),
        name="saddle",
    )(
        *[
            pltpu.with_memory_space_constraint(operand, pltpu.HBM)
            for operand in (
                jnp.swapaxes(obs_sites, 0, 1), obs_dual.reshape(pair), obs_variance.reshape(pair),
                diffusion, drift_rows, drift_cols, spread, row_factor, col_factor,
                layer_in.T, bias_in.reshape(1, hidden), layer_out,
                increment[0], multiplier[0], trajectory[0],
            )
        ]
    )
    return (before - ahead)[None], seen.reshape(1, own), mult_out[None]


def solution(mesh):
    placed = (
        P("win", "space", None, None), P("win", "space", None, None), P("win", "space"),
        P("win", None, None), P("win", "space"), P("win", None, "space", None),
        P(), P(), P(), P(), P(), P(), P(), P(), P(),
    )
    return jax.shard_map(
        body,
        mesh=mesh,
        in_specs=placed,
        out_specs=(P("win", "space", None, None), P("win", "space"), P("win", "space", None, None)),
        check_vma=False,
    )
```

time: 124 us -> 115 us (0.927)
  local copies, waits for them, and re-layouts: 6.59 us -> 1.56 us
  Pallas kernels: 116 us -> 112 us
    unnamed x11 -> x2, local copies, waits for them, and re-layouts: 6.59 us -> 1.56 us
    pallas_call x1, Pallas kernels: 116 us -> 112 us  [body(): pl.pallas_call(kernel, out_shape=(full, full, jax.ShapeDtypeStruct(pair,...]
where the time goes in v2:
time: 115 us
  Pallas kernels  112 us (97%)
  local copies, waits for them, and re-layouts  1.56 us (1%)
    pallas_call x1, Pallas kernels, body(): pl.pallas_call(kernel, out_shape=(full, full, jax.ShapeDtypeStruct(pair,...  112 us

profile of v2, /device:TPU:25, one launch (start us, length us, event | category | flops | bytes accessed | tf_op | source)
XLA Modules:
  0.0 114.9 jit_solution(2404162014850220948)
XLA Ops:
  0.6 111.5 %saddle.1 = (f32[4,256,256]{2,1,0:T(8,128)S(1)}, f32[4,256,256]{2,1,0:T(8,128)S(1)}, f32[2,1,512]{2,1,0:T(1,128)S(1)}, f32[4,256,256]{2,1,0:T(8,128)S(1)}) custom-call(s32[3,1,16384]{2,1,0:T(1,128)} %bitcast.17, f32[2,1,512]{2,1,0:T(1,128)} %bitcast.19, f32[2,1,512]{2,1,0:T(1,128)} %bitcast.20, f32[64]{0:T(128)} %diffusion_any.1, f32[64]{0:T(128)} %drift_rows_any.1, ...), custom_call_target="tpu_custom_call" | custom-call | tf_op jit(solution)/shard_map/saddle/pallas_call | solution.py:453
  112.2 1.1 subtract_bitcast_fusion
  113.3 0.6 copy.20
  113.9 1.0 copy.21

commit v3 on v2

--- a/solution.py
+++ b/solution.py
@@ -41,25 +41,30 @@
     return dot(a[0], b[0]) + (dot(a[0], b[1]) + dot(a[1], b[0]))
 
 
-def stencil(field, diffusion, drift_rows, drift_cols, direction):
-    rows, cols = field.shape
-    edge = 8
-    row_id = lax.broadcasted_iota(jnp.int32, (edge, cols), 0)
-    col_id = lax.broadcasted_iota(jnp.int32, (1, cols), 1)
+def stencil(field, pads, diffusion, drift_rows, drift_cols, direction):
+    rows = field.shape[0]
+    edge = (pads.shape[2] - rows) // 2
+    lane = lax.broadcasted_iota(jnp.int32, (1, LANES), 1)
+    first, last = lane == 0, lane == LANES - 1
     centre = 1.0 - 4.0 * diffusion
     row_up, row_dn = diffusion - direction * drift_rows, diffusion + direction * drift_rows
-    col_up = jnp.where(col_id == cols - 1, 0.0, diffusion - direction * drift_cols)
-    col_dn = jnp.where(col_id == 0, 0.0, diffusion + direction * drift_cols)
-    for _ in range(STEPS):
-        up1 = pltpu.roll(field, rows - 1, 0)
-        last = jnp.where(row_id == edge - 1, 0.0, up1[rows - edge :])
-        up1 = jnp.concatenate([up1[: rows - edge], last], 0)
-        dn1 = pltpu.roll(field, 1, 0)
-        dn1 = jnp.concatenate([jnp.where(row_id == 0, 0.0, dn1[:edge]), dn1[edge:]], 0)
-        up2 = pltpu.roll(field, cols - 1, 1)
-        dn2 = pltpu.roll(field, 1, 1)
-        field = centre * field + (row_up * up1 + row_dn * dn1) + (col_up * up2 + col_dn * dn2)
-    return field
+    col_up, col_dn = diffusion - direction * drift_cols, diffusion + direction * drift_cols
+    up_end, dn_end = jnp.where(last, 0.0, col_up), jnp.where(first, 0.0, col_dn)
+    parts = [field[:, :LANES], field[:, LANES:]]
+    for step in range(STEPS):
+        rows_of = []
+        for h in range(2):
+            page = pads.at[step % 2, h]
+            page[edge : edge + rows, :] = parts[h]
+            up1, dn1 = page[edge + 1 : edge + 1 + rows, :], page[edge - 1 : edge - 1 + rows, :]
+            rows_of.append(centre * parts[h] + (row_up * up1 + row_dn * dn1))
+        ups = [pltpu.roll(part, LANES - 1, 1) for part in parts]
+        downs = [pltpu.roll(part, 1, 1) for part in parts]
+        parts = [
+            rows_of[0] + (col_up * jnp.where(last, ups[1], ups[0]) + dn_end * downs[0]),
+            rows_of[1] + (up_end * ups[1] + col_dn * jnp.where(first, downs[0], downs[1])),
+        ]
+    return jnp.concatenate(parts, 1)
 
 
 def kernel(
@@ -69,7 +74,7 @@
     sites, dual, variance, diffusion, drift_rows, drift_cols, spread, row_factor, col_factor,
     w_in_t, bias, w_out, inc, mult, traj,
     stepped, path, strip_m, strip_i, slopes, out_b, out_f, slab_b,
-    before, placed, picked, w_path, w_tangent, w_adjoint, duals, seen, seen_in, outm, obs,
+    before, placed, picked, w_path, w_tangent, w_adjoint, duals, seen, seen_in, outm, obs, pads,
     load_sem, store_sem, m_send, m_recv, i_send, i_recv, b_send, b_recv, f_send, f_recv,
     d_send, d_recv, s_send, s_recv, keep_sem, level_sem,
 ):
@@ -206,13 +211,14 @@
                 mult_copy(p, c).start()
             keep_mult(c).start()
 
+    pads[...] = jnp.zeros_like(pads)
     for load in loads[0:4]:
         load.wait()
 
     def step_forward(level, carry):
         at = first + level
         stepped[level] = stencil(
-            inc[level], diffusion[at], drift_rows[at], drift_cols[at], 1.0
+            inc[level], pads, diffusion[at], drift_rows[at], drift_cols[at], 1.0
         )
         return carry
 
@@ -220,9 +226,13 @@
 
     @pl.when(has_after)
     def _():
-        for c in range(chunks):
-            for p in everyone:
-                inc_copy(p, c).start()
+        for p in everyone:
+            inc_copy(p, 0).start()
+
+    @pl.when(has_after)
+    def _():
+        for p in everyone:
+            inc_copy(p, 1).start()
 
     for load in loads[4:8]:
         load.wait()
@@ -261,7 +271,7 @@
             slopes[at, part, :] = (1.0 + bend) * (1.0 + half_act * (1.0 - bend))
         return carry
 
-    lax.fori_loop(0, chunks * strip // 2, slope_rows, 0)
+    lax.fori_loop(0 * strip // 2, (0 + 1) * strip // 2, slope_rows, 0)
 
     def network(source, target, w_first, w_second):
         def visit(at, carry):
@@ -282,30 +292,6 @@
 
         return visit
 
-    for load in loads[8:]:
-        load.wait()
-    exact = lax.Precision.HIGHEST
-    left = split_two(dot_nt(row_factor[...], row_factor[...], exact))
-    right = split_two(dot_nt(col_factor[...], col_factor[...], exact))
-
-    def correlate(level, carry):
-        scale = spread[first + level]
-        inner = split_two(dot_three(left, split_two(mult[level])))
-        before[level] = (scale * scale) * dot_three(inner, right) + inc[level]
-        return carry
-
-    lax.fori_loop(0, depth, correlate, 0)
-    store_before = pltpu.make_async_copy(before, before_any, store_sem.at[0])
-    store_before.start()
-
-    for level in range(depth):
-        high, low = split_two(inc[level].T)
-        part = slice(level * rows, (level + 1) * rows)
-        picked[0:cols, part] = high
-        picked[cols : 2 * cols, part] = low
-    placed[...] = jnp.zeros_like(placed)
-    keep_dual.wait()
-    all_dual.wait_recv()
     row_ids = lax.broadcasted_iota(jnp.int32, (depth * rows, BLOCK), 0)
     col_ids = lax.broadcasted_iota(jnp.int32, (cols, BLOCK), 0)
 
@@ -329,34 +315,82 @@
         return carry
 
     blocks = sites.shape[2] // BLOCK
-    cuts = [blocks * k // 32 for k in (0, 4, 13, 20, 32)]
+    cuts = [blocks * k // 32 for k in (0, 0, 12, 20, 32)]
 
     adjoint = network(strip_m, out_b, w_adjoint, w_in_t)
     tangent = network(strip_i, out_f, w_tangent, w_out)
 
-    for c in range(chunks):
-
-        @pl.when(has_prior)
-        def _():
-            keep_mult(c).wait()
-            all_mult(c).wait_recv()
-            lax.fori_loop(c * strip // 2, (c + 1) * strip // 2, adjoint, 0)
-            for p in everyone:
-                back_copy(p, c).start()
-
-        lax.fori_loop(cuts[c], cuts[c + 1], observe, 0)
-
-    for c in range(chunks):
-
-        @pl.when(has_prior)
-        def _():
-            all_inc(c).wait_recv()
-            lax.fori_loop(c * strip // 2, (c + 1) * strip // 2, tangent, 0)
-            for p in PARTNERS:
-                ahead_copy(p, c).start()
-            keep_ahead(c).start()
-
-        lax.fori_loop(cuts[2 + c], cuts[3 + c], observe, 0)
+    @pl.when(has_prior)
+    def _():
+        keep_mult(0).wait()
+        all_mult(0).wait_recv()
+        lax.fori_loop(0 * strip // 2, (0 + 1) * strip // 2, adjoint, 0)
+        for p in everyone:
+            back_copy(p, 0).start()
+
+    lax.fori_loop(1 * strip // 2, (1 + 1) * strip // 2, slope_rows, 0)
+    for load in loads[8:]:
+        load.wait()
+    exact = lax.Precision.HIGHEST
+    left = split_two(dot_nt(row_factor[...], row_factor[...], exact))
+    right = split_two(dot_nt(col_factor[...], col_factor[...], exact))
+
+    def correlate(level, carry):
+        scale = spread[first + level]
+        inner = split_two(dot_three(left, split_two(mult[level])))
+        before[level] = (scale * scale) * dot_three(inner, right) + inc[level]
+        return carry
+
+    lax.fori_loop(0, depth, correlate, 0)
+    store_before = pltpu.make_async_copy(before, before_any, store_sem.at[0])
+    store_before.start()
+
+    for level in range(depth):
+        high, low = split_two(inc[level].T)
+        part = slice(level * rows, (level + 1) * rows)
+        picked[0:cols, part] = high
+        picked[cols : 2 * cols, part] = low
+    placed[...] = jnp.zeros_like(placed)
+    keep_dual.wait()
+    all_dual.wait_recv()
+    @pl.when(has_prior)
+    def _():
+        keep_mult(1).wait()
+        all_mult(1).wait_recv()
+        lax.fori_loop(1 * strip // 2, (1 + 1) * strip // 2, adjoint, 0)
+        for p in everyone:
+            back_copy(p, 1).start()
+
+    lax.fori_loop(cuts[1], cuts[2], observe, 0)
+
+
+    @pl.when(has_prior)
+    def _():
+        all_inc(0).wait_recv()
+        lax.fori_loop(0 * strip // 2, (0 + 1) * strip // 2, tangent, 0)
+
+    @pl.when(has_prior)
+    def _():
+        for p in PARTNERS:
+            ahead_copy(p, 0).start()
+        keep_ahead(0).start()
+
+    lax.fori_loop(12, 20, observe, 0)
+
+    @pl.when(has_prior)
+    def _():
+        all_inc(1).wait_recv()
+        lax.fori_loop(1 * strip // 2, (1 + 1) * strip // 2, tangent, 0)
+
+    lax.fori_loop(20, 24, observe, 0)
+
+    @pl.when(has_prior)
+    def _():
+        for p in PARTNERS:
+            ahead_copy(p, 1).start()
+        keep_ahead(1).start()
+
+    lax.fori_loop(24, 32, observe, 0)
 
     def store_mult(level):
         return pltpu.make_async_copy(outm.at[level], mult_out_any.at[level], level_sem.at[level])
@@ -376,7 +410,7 @@
 
         def step_back(level, carry):
             at = first + level
-            later = stencil(slab_b[level], diffusion[at], drift_rows[at], drift_cols[at], -1.0)
+            later = stencil(slab_b[level], pads, diffusion[at], drift_rows[at], drift_cols[at], -1.0)
             outm[level] = add_placed(level) - later
             store_mult(level).start()
             return carry
@@ -431,6 +465,24 @@
         blank = pltpu.make_async_copy(stepped, slab_f, store_sem.at[3])
         blank.start()
         blank.wait()
+
+
+def finish(before, ahead, obs_any, mult_any, state_out, obs_out, mult_out, state, sem):
+    depth = state.shape[0]
+    copies = [
+        pltpu.make_async_copy(mult_any, mult_out.at[0], sem.at[depth]),
+        pltpu.make_async_copy(obs_any, obs_out.at[0], sem.at[depth + 1]),
+    ]
+    for copy in copies:
+        copy.start()
+    for level in range(depth):
+        state[level] = before[level] - ahead[level]
+        copies.append(
+            pltpu.make_async_copy(state.at[level], state_out.at[0, level], sem.at[level])
+        )
+        copies[-1].start()
+    for copy in copies:
+        copy.wait()
 
 
 def body(
@@ -482,6 +534,7 @@
             pltpu.VMEM((spaces,) + pair, F32),
             slab,
             pltpu.VMEM(pair, F32),
+            pltpu.VMEM((2, 2, rows + 16, LANES), F32),
             dma((15,)), dma((4,)),
             *[dma((chunks,))] * 8,
             *[dma] * 4,
@@ -502,7 +555,20 @@
             )
         ]
     )
-    return (before - ahead)[None], seen.reshape(1, own), mult_out[None]
+    state_out, obs_out, mult_out = pl.pallas_call(
+        finish,
+        out_shape=(
+            jax.ShapeDtypeStruct(increment.shape, F32),
+            jax.ShapeDtypeStruct((1, own // BLOCK, 1, BLOCK), F32),
+            jax.ShapeDtypeStruct(increment.shape, F32),
+        ),
+        in_specs=[pl.BlockSpec(memory_space=pltpu.VMEM)] * 2 + [anywhere] * 2,
+        out_specs=(anywhere,) * 3,
+        scratch_shapes=[slab, dma((depth + 2,))],
+        compiler_params=pltpu.CompilerParams(vmem_limit_bytes=8 * 1024 * 1024),
+        name="finish",
+    )(before, ahead, seen, mult_out)
+    return state_out, obs_out.reshape(1, own), mult_out
 
 
 def solution(mesh):

time: 115 us -> 113 us (0.983)
  local copies, waits for them, and re-layouts: 1.56 us -> 0 us
    unnamed x2 -> x0, local copies, waits for them, and re-layouts: 1.56 us -> none
    pallas_call x0 -> x1, Pallas kernels: none -> 1.36 us  [body(): pl.pallas_call(finish, out_shape=(jax.ShapeDtypeStruct(increment.shape, F...]
where the time goes in v3:
time: 113 us
  Pallas kernels  112 us (99%)
    pallas_call x1, Pallas kernels, body(): pl.pallas_call(kernel, out_shape=(full, full, jax.ShapeDtypeStruct(pair,...  111 us

profile of v3, /device:TPU:25, one launch (start us, length us, event | category | flops | bytes accessed | tf_op | source)
XLA Modules:
  0.0 113.0 jit_solution(168732145269360885)
XLA Ops:
  0.6 111.0 %saddle.1 = (f32[4,256,256]{2,1,0:T(8,128)S(1)}, f32[4,256,256]{2,1,0:T(8,128)S(1)}, f32[2,1,512]{2,1,0:T(1,128)S(1)}, f32[4,256,256]{2,1,0:T(8,128)S(1)}) custom-call(s32[3,1,16384]{2,1,0:T(1,128)} %bitcast.12, f32[2,1,512]{2,1,0:T(1,128)} %bitcast.14, f32[2,1,512]{2,1,0:T(1,128)} %bitcast.15, f32[64]{0:T(128)} %diffusion_any.1, f32[64]{0:T(128)} %drift_rows_any.1, ...), custom_call_target="tpu_custom_call" | custom-call | tf_op jit(solution)/shard_map/saddle/pallas_call | solution.py:505
  111.7 1.4 %finish.1 = (f32[1,4,256,256]{3,2,1,0:T(8,128)}, f32[1,2,1,512]{3,2,1,0:T(1,128)}, f32[1,4,256,256]{3,2,1,0:T(8,128)}) custom-call(f32[4,256,256]{2,1,0:T(8,128)S(1)} %get-tuple-element.10.before, f32[4,256,256]{2,1,0:T(8,128)S(1)} %get-tuple-element.11.ahead, f32[2,1,512]{2,1,0:T(1,128)S(1)} %get-tuple-element.12.obs_any, ...), custom_call_target="tpu_custom_call" | custom-call | tf_op jit(solution)/shard_map/finish/pallas_call | solution.py:558

commit v4 on v3

--- a/solution.py
+++ b/solution.py
@@ -10,6 +10,7 @@
 F32, BF16 = jnp.float32, jnp.bfloat16
 PARTNERS = (8, 12, 10, 14, 9, 13, 11, 15, 4, 6, 2, 5, 7, 3, 1)
 BLOCK = 512
+GROUPS = 4
 LANES = 128
 VMEM_LIMIT = 44 * 1024 * 1024
 
@@ -86,6 +87,7 @@
     wins = lax.axis_size("win")
     after, prior = lax.rem(w + 1, wins), lax.rem(w + wins - 1, wins)
     first = s * depth
+    group = depth // GROUPS
 
     barrier = pltpu.get_barrier_semaphore()
     for p in PARTNERS + (0,):
@@ -143,11 +145,12 @@
             i_send.at[c], i_recv.at[c], after, d,
         )
 
-    def back_copy(p, c):
+    def back_copy(p, c, g):
         d = flip(s, p)
         return remote(
-            out_b.at[c, depth_of(d)], slab_b.at[:, strip_of(s), chunk_of(c)],
-            b_send.at[c], b_recv.at[c], prior, d,
+            out_b.at[c, pl.ds(d * depth + g * group, group)],
+            slab_b.at[pl.ds(g * group, group), strip_of(s), chunk_of(c)],
+            b_send.at[g, c], b_recv.at[g, c], prior, d,
         )
 
     def ahead_copy(p, c):
@@ -189,8 +192,9 @@
     def all_inc(c):
         return all_of(strip_i.at[c], i_send.at[c], i_recv.at[c])
 
-    def all_back(c):
-        return all_of(out_b.at[c], b_send.at[c], b_recv.at[c])
+    def all_back(c, g):
+        part = out_b.at[c, pl.ds(0, spaces * group)]
+        return all_of(part, b_send.at[g, c], b_recv.at[g, c])
 
     def all_ahead(c):
         return all_of(out_f.at[c, pl.ds(0, others * depth)], f_send.at[c], f_recv.at[c])
@@ -325,8 +329,9 @@
         keep_mult(0).wait()
         all_mult(0).wait_recv()
         lax.fori_loop(0 * strip // 2, (0 + 1) * strip // 2, adjoint, 0)
-        for p in everyone:
-            back_copy(p, 0).start()
+        for g in range(GROUPS):
+            for p in everyone:
+                back_copy(p, 0, g).start()
 
     lax.fori_loop(1 * strip // 2, (1 + 1) * strip // 2, slope_rows, 0)
     for load in loads[8:]:
@@ -358,8 +363,9 @@
         keep_mult(1).wait()
         all_mult(1).wait_recv()
         lax.fori_loop(1 * strip // 2, (1 + 1) * strip // 2, adjoint, 0)
-        for p in everyone:
-            back_copy(p, 1).start()
+        for g in range(GROUPS):
+            for p in everyone:
+                back_copy(p, 1, g).start()
 
     lax.fori_loop(cuts[1], cuts[2], observe, 0)
 
@@ -382,7 +388,7 @@
         all_inc(1).wait_recv()
         lax.fori_loop(1 * strip // 2, (1 + 1) * strip // 2, tangent, 0)
 
-    lax.fori_loop(20, 24, observe, 0)
+    lax.fori_loop(20, 27, observe, 0)
 
     @pl.when(has_prior)
     def _():
@@ -390,7 +396,7 @@
             ahead_copy(p, 1).start()
         keep_ahead(1).start()
 
-    lax.fori_loop(24, 32, observe, 0)
+    lax.fori_loop(27, 32, observe, 0)
 
     def store_mult(level):
         return pltpu.make_async_copy(outm.at[level], mult_out_any.at[level], level_sem.at[level])
@@ -405,8 +411,6 @@
 
     @pl.when(has_after)
     def _():
-        for c in range(chunks):
-            all_back(c).wait_recv()
 
         def step_back(level, carry):
             at = first + level
@@ -415,7 +419,10 @@
             store_mult(level).start()
             return carry
 
-        lax.fori_loop(0, depth, step_back, 0)
+        for g in range(GROUPS):
+            for c in range(chunks):
+                all_back(c, g).wait_recv()
+            lax.fori_loop(g * group, (g + 1) * group, step_back, 0)
 
     @pl.when(w == wins - 1)
     def _():
@@ -444,7 +451,8 @@
     @pl.when(has_prior)
     def _():
         for c in range(chunks):
-            all_back(c).wait_send()
+            for g in range(GROUPS):
+                all_back(c, g).wait_send()
             all_mult(c).wait_send()
 
     for level in range(depth):
@@ -536,7 +544,9 @@
             pltpu.VMEM(pair, F32),
             pltpu.VMEM((2, 2, rows + 16, LANES), F32),
             dma((15,)), dma((4,)),
-            *[dma((chunks,))] * 8,
+            *[dma((chunks,))] * 4,
+            *[dma((GROUPS, chunks))] * 2,
+            *[dma((chunks,))] * 2,
             *[dma] * 4,
             dma((2 + 2 * chunks,)), dma((depth,)),
         ],

time: 113 us -> 111 us (0.982)
  the two profiles are of different devices: /device:TPU:25 before, /device:TPU:17 now
where the time goes in v4:
time: 111 us
  Pallas kernels  110 us (99%)
    pallas_call x1, Pallas kernels, body(): pl.pallas_call(kernel, out_shape=(full, full, jax.ShapeDtypeStruct(pair,...  109 us

profile of v4, /device:TPU:17, one launch (start us, length us, event | category | flops | bytes accessed | tf_op | source)
XLA Modules:
  0.0 110.7 jit_solution(2184692920440739442)
XLA Ops:
  0.6 108.5 %saddle.1 = (f32[4,256,256]{2,1,0:T(8,128)S(1)}, f32[4,256,256]{2,1,0:T(8,128)S(1)}, f32[2,1,512]{2,1,0:T(1,128)S(1)}, f32[4,256,256]{2,1,0:T(8,128)S(1)}) custom-call(s32[3,1,16384]{2,1,0:T(1,128)} %bitcast.12, f32[2,1,512]{2,1,0:T(1,128)} %bitcast.14, f32[2,1,512]{2,1,0:T(1,128)} %bitcast.15, f32[64]{0:T(128)} %diffusion_any.1, f32[64]{0:T(128)} %drift_rows_any.1, ...), custom_call_target="tpu_custom_call" | custom-call | tf_op jit(solution)/shard_map/saddle/pallas_call | solution.py:513
  109.2 1.4 %finish.1 = (f32[1,4,256,256]{3,2,1,0:T(8,128)}, f32[1,2,1,512]{3,2,1,0:T(1,128)}, f32[1,4,256,256]{3,2,1,0:T(8,128)}) custom-call(f32[4,256,256]{2,1,0:T(8,128)S(1)} %get-tuple-element.10.before, f32[4,256,256]{2,1,0:T(8,128)S(1)} %get-tuple-element.11.ahead, f32[2,1,512]{2,1,0:T(1,128)S(1)} %get-tuple-element.12.obs_any, ...), custom_call_target="tpu_custom_call" | custom-call | tf_op jit(solution)/shard_map/finish/pallas_call | solution.py:568

commit v5 on v4

--- a/solution.py
+++ b/solution.py
@@ -205,8 +205,6 @@
     has_prior, has_after = w > 0, w < wins - 1
 
     keep_dual.start()
-    for p in PARTNERS:
-        dual_copy(p).start()
 
     @pl.when(has_prior)
     def _():
@@ -214,6 +212,9 @@
             for p in PARTNERS:
                 mult_copy(p, c).start()
             keep_mult(c).start()
+
+    for p in PARTNERS:
+        dual_copy(p).start()
 
     pads[...] = jnp.zeros_like(pads)
     for load in loads[0:4]:

time: 111 us -> 111 us (level)
  the two profiles are of different devices: /device:TPU:17 before, /device:TPU:25 now
where the time goes in v5:
time: 111 us
  Pallas kernels  110 us (99%)
    pallas_call x1, Pallas kernels, body(): pl.pallas_call(kernel, out_shape=(full, full, jax.ShapeDtypeStruct(pair,...  108 us

profile of v5, /device:TPU:25, one launch (start us, length us, event | category | flops | bytes accessed | tf_op | source)
XLA Modules:
  0.0 110.6 jit_solution(526279289039333025)
XLA Ops:
  0.6 108.5 %saddle.1 = (f32[4,256,256]{2,1,0:T(8,128)S(1)}, f32[4,256,256]{2,1,0:T(8,128)S(1)}, f32[2,1,512]{2,1,0:T(1,128)S(1)}, f32[4,256,256]{2,1,0:T(8,128)S(1)}) custom-call(s32[3,1,16384]{2,1,0:T(1,128)} %bitcast.12, f32[2,1,512]{2,1,0:T(1,128)} %bitcast.14, f32[2,1,512]{2,1,0:T(1,128)} %bitcast.15, f32[64]{0:T(128)} %diffusion_any.1, f32[64]{0:T(128)} %drift_rows_any.1, ...), custom_call_target="tpu_custom_call" | custom-call | tf_op jit(solution)/shard_map/saddle/pallas_call | solution.py:514
  109.1 1.4 %finish.1 = (f32[1,4,256,256]{3,2,1,0:T(8,128)}, f32[1,2,1,512]{3,2,1,0:T(1,128)}, f32[1,4,256,256]{3,2,1,0:T(8,128)}) custom-call(f32[4,256,256]{2,1,0:T(8,128)S(1)} %get-tuple-element.10.before, f32[4,256,256]{2,1,0:T(8,128)S(1)} %get-tuple-element.11.ahead, f32[2,1,512]{2,1,0:T(1,128)S(1)} %get-tuple-element.12.obs_any, ...), custom_call_target="tpu_custom_call" | custom-call | tf_op jit(solution)/shard_map/finish/pallas_call | solution.py:569
